TPU v7x, 32 devices: a whole 2x2x4 slice. The times are simulated.
32 devices in a mesh: wide: 4 (over z), narrow: 8 (over y, x, core).
Axes of the slice: x: 2, y: 2, z: 4, core: 2. Of those that a mesh axis runs over, the one named last changes fastest.
Arguments:
- phase_ids: int32 [512, 512, 256], P('wide', 'narrow'), may hold values from 0 to 3
- conduct_table: float32 [4, 3], replicated, may hold values from 0.2 to 5
- gradient: float32 [3], replicated, may hold values from -3 to 3
- start_field: float32 [512, 512, 256], P('wide', 'narrow'), may hold values from -32 to 32
Outputs:
- solution: float32 [512, 512, 256], P('wide', 'narrow')
- residual_next: float32 [512, 512, 256], P('wide', 'narrow')
- new_direction: float32 [512, 512, 256], P('wide', 'narrow')
Inputs may be any that keep to these rules, and one draw needn't show every extreme that they name: `phase_ids`: each voxel's phase indexes a row of conduct_table.
All inputs are finite; a program needn't handle non-finite values.
Results may differ from a plain program's by a relative error of at most 0.0065.
Values sent between devices are 32-bit elements; how exact they have to be, the bound alone decides.
No kernel may reach another device: no remote copies, remote signals or barrier semaphores. Data moves between devices by JAX's collectives and lax.ppermute only.
A program may use at most 256 MiB of HBM per device.

v0:
```python
import jax
import jax.numpy as jnp
from jax import lax
from jax.sharding import PartitionSpec as P

NX = 512
NY = 512
NZ = 256
PHASES = 4


HIGHEST = lax.Precision.HIGHEST
FORWARD_FORMS = ("nyz,mn->myz", "xnz,mn->xmz", "xyn,mn->xym")
INVERSE_FORMS = ("myz,mn->nyz", "xmz,mn->xnz", "xym,mn->xyn")


def extended(shard, sides, width):
    for axis, dim in sides:
        devices, length = (lax.axis_size(axis), shard.shape[dim])
        up = [(i, (i + 1) % devices) for i in range(devices - 1)]
        down = [(j, i) for i, j in up]
        last = lax.slice_in_dim(shard, length - width, length, axis=dim)
        initial = lax.slice_in_dim(shard, 0, width, axis=dim)
        before = lax.ppermute(last, axis, up)
        after = lax.ppermute(initial, axis, down)
        shard = jnp.concatenate([before, shard, after], axis=dim)
    return shard


def cosine_table(length):
    freq_index = jnp.arange(length, dtype=jnp.int32)[:, None]
    cell_index = jnp.arange(length, dtype=jnp.int32)[None, :]
    wrapped = freq_index * (2 * cell_index + 1) % (4 * length)
    angle_rad = wrapped.astype(jnp.float32) * (jnp.pi / (2.0 * length))
    weight = jnp.where(
        freq_index == 0, jnp.sqrt(jnp.float32(1.0 / length)), jnp.sqrt(jnp.float32(2.0 / length))
    )
    return weight * jnp.cos(angle_rad)


def eigen_values(length, index):
    angle_rad = index.astype(jnp.float32) * (jnp.pi / length)
    return 2.0 - 2.0 * jnp.cos(angle_rad)


def green_block(base_cond, index_x, index_y, index_z):
    lowest = eigen_values(NX, jnp.ones((), jnp.int32))
    eigen_sum = lowest + eigen_values(NX, index_x)[:, None, None]
    eigen_sum = eigen_sum + eigen_values(NY, index_y)[None, :, None]
    eigen_sum = eigen_sum + eigen_values(NZ, index_z)[None, None, :]
    zero_mode = (
        (index_x[:, None, None] == 0)
        & (index_y[None, :, None] == 0)
        & (index_z[None, None, :] == 0)
    )
    return jnp.where(zero_mode, jnp.float32(0.0), 1.0 / (base_cond * eigen_sum))


def transform(values, matrix, axis_dim, inverse):
    einsum_form = INVERSE_FORMS[axis_dim] if inverse else FORWARD_FORMS[axis_dim]
    return jnp.einsum(einsum_form, values, matrix, precision=HIGHEST)


def harmonic(lower_side, upper_side):
    return 2.0 * lower_side * upper_side / (lower_side + upper_side)


def conductivities(phase_ids, conduct_table):
    result = []
    for component in range(3):
        summed = jnp.zeros(phase_ids.shape, jnp.float32)
        for member in range(PHASES):
            summed = summed + jnp.where(
                phase_ids == member, conduct_table[member, component], jnp.float32(0.0)
            )
        result.append(summed)
    return result


def pad_depth(values):
    return jnp.pad(values, ((0, 0), (0, 0), (1, 1)))


def apply_padded(field_pad, faces):
    inner_x = field_pad[:, 1:-1, :]
    flux_x = faces[0] * (inner_x[1:] - inner_x[:-1])
    inner_y = field_pad[1:-1, :, :]
    flux_y = faces[1] * (inner_y[:, 1:] - inner_y[:, :-1])
    inner_z = pad_depth(field_pad[1:-1, 1:-1, :])
    flux_z = faces[2] * (inner_z[:, :, 1:] - inner_z[:, :, :-1])
    divergence = flux_x[1:] - flux_x[:-1] + (flux_y[:, 1:] - flux_y[:, :-1])
    divergence = divergence + (flux_z[:, :, 1:] - flux_z[:, :, :-1])
    return -divergence


def precondition(grid_field, tables, base_cond):
    table_x, table_y, table_z = tables
    spectral = transform(grid_field, table_z, 2, False)
    spectral = transform(
        lax.all_to_all(spectral, "narrow", split_axis=2, concat_axis=1, tiled=True),
        table_y,
        1,
        False,
    )
    spectral = transform(
        lax.all_to_all(spectral, "wide", split_axis=1, concat_axis=0, tiled=True), table_x, 0, False
    )
    count_y = spectral.shape[1]
    count_z = spectral.shape[2]
    index_x = jnp.arange(NX, dtype=jnp.int32)
    index_y = lax.axis_index("wide") * count_y + jnp.arange(count_y, dtype=jnp.int32)
    index_z = lax.axis_index("narrow") * count_z + jnp.arange(count_z, dtype=jnp.int32)
    spectral = spectral * green_block(base_cond, index_x, index_y, index_z)
    spectral = transform(spectral, table_x, 0, True)
    spectral = transform(
        lax.all_to_all(spectral, "wide", split_axis=0, concat_axis=1, tiled=True), table_y, 1, True
    )
    return transform(
        lax.all_to_all(spectral, "narrow", split_axis=1, concat_axis=2, tiled=True),
        table_z,
        2,
        True,
    )


def on_device(phase_ids, conduct_table, gradient, start_field):
    cond_x, cond_y, cond_z = conductivities(phase_ids, conduct_table)
    stacked = jnp.stack([start_field, cond_x, cond_y])
    padded = extended(stacked, (("wide", 1), ("narrow", 2)), 1)
    start_pad = padded[0]
    cond_xp = padded[1][:, 1:-1, :]
    cond_yp = padded[2][1:-1, :, :]
    cond_zp = pad_depth(cond_z)
    faces = (
        harmonic(cond_xp[:-1], cond_xp[1:]),
        harmonic(cond_yp[:, :-1], cond_yp[:, 1:]),
        harmonic(cond_zp[:, :, :-1], cond_zp[:, :, 1:]),
    )
    source = gradient[0] * (faces[0][1:] - faces[0][:-1])
    source = source + gradient[1] * (faces[1][:, 1:] - faces[1][:, :-1])
    source = source + gradient[2] * (faces[2][:, :, 1:] - faces[2][:, :, :-1])
    residual = source - apply_padded(start_pad, faces)
    tables = (cosine_table(NX), cosine_table(NY), cosine_table(NZ))
    base_cond = jnp.mean(conduct_table)
    direction = precondition(residual, tables, base_cond)
    direction_pad = extended(direction, (("wide", 0), ("narrow", 1)), 1)
    image_field = apply_padded(direction_pad, faces)
    rz_now = lax.psum(jnp.sum(residual * direction), ("wide", "narrow"))
    curvature = lax.psum(jnp.sum(direction * image_field), ("wide", "narrow"))
    step_alpha = rz_now / curvature
    solution = start_field + step_alpha * direction
    residual_next = residual - step_alpha * image_field
    preconditioned = precondition(residual_next, tables, base_cond)
    rz_next = lax.psum(jnp.sum(residual_next * preconditioned), ("wide", "narrow"))
    new_direction = preconditioned + rz_next / rz_now * direction
    return (solution, residual_next, new_direction)


def solution(mesh):
    placed = (P("wide", "narrow", None), P(), P(), P("wide", "narrow", None))
    return jax.shard_map(
        on_device,
        mesh=mesh,
        in_specs=placed,
        out_specs=(P("wide", "narrow", None), P("wide", "narrow", None), P("wide", "narrow", None)),
        check_vma=False,
    )
```

profile of v0, /device:TPU:0, one launch (start us, length us, event | category | flops | bytes accessed | tf_op | source)
XLA Modules:
  0.0 1928.2 jit_solution(9255614372349274259)
XLA Ops:
  98.6 19.2 fusion.4
  117.8 19.0 fusion.8
  136.8 22.0 %fusion.1 = (f32[128,64,257]{2,0,1:T(8,128)}, f32[128,64,257]{2,0,1:T(8,128)}) fusion(f32[128,64,256]{2,0,1:T(8,128)} %slice.296, f32[128,64,256]{2,0,1:T(8,128)} %get-tuple-element.45), kind=kLoop, calls=%fused_computation.8 | loop fusion | flops 12632064 | bytes 33619968 | tf_op jit(solution)/shard_map/mul | solution.py:90
  158.8 41.1 %fusion.14 = f32[128,64,256]{2,0,1:T(8,128)} fusion(f32[128,64,257]{2,0,1:T(8,128)} %get-tuple-element.24, f32[128,65,256]{2,0,1:T(8,128)} %get-tuple-element.22, f32[129,64,256]{2,0,1:T(8,128)} %get-tuple-element.20, f32[128,64,257]{2,0,1:T(8,128)} %get-tuple-element.25, f32[128,65,256]{2,0,1:T(8,128)} %get-tuple-element.23, ...), kind=kLoop, calls=%fused_computation.41 | loop fusion | flops 31457280 | bytes 109051920 | tf_op jit(solution)/shard_map/sub | solution.py:142
  231.8 94.1 %all-to-all-done = f32[128,64,256]{0,1,2:T(8,128)} async-done(((f32[128,64,256]{0,1,2:T(8,128)}), f32[128,64,256]{0,1,2:T(8,128)}, u32[]{:S(2)}, u32[]{:S(2)}) %all-to-all-start) | async-done | bytes 8388640 | tf_op jit(solution)/shard_map/all_to_all | solution.py:100
  334.1 29.1 %fusion.43 = f32[128,512,32]{0,1,2:T(8,128)S(1)} fusion(f32[128,512,32]{0,2,1:T(8,128)S(1)} %bitcast.111, s32[512]{0:T(512)S(1)} %multiply_add_fusion.2, f32[512]{0:T(512)S(1)} %broadcast_select_fusion), kind=kOutput, calls=%fused_computation.92 | convolution fusion | flops 12888834048 | bytes 16781312 | tf_op jit(solution)/shard_map/xnz,mn->xmz/dot_general | solution.py:61
  379.0 179.1 %all-to-all-done.1 = f32[128,512,32]{0,2,1:T(8,128)} async-done(((f32[128,512,32]{0,2,1:T(8,128)}), f32[128,512,32]{0,2,1:T(8,128)}, u32[]{:S(2)}, u32[]{:S(2)}) %all-to-all-start.1) | async-done | bytes 8388640 | tf_op jit(solution)/shard_map/all_to_all | solution.py:106
  568.0 22.5 %fusion.62 = f32[512,128,32]{1,0,2:T(8,128)S(1)} fusion(f32[512,128,32]{1,0,2:T(8,128)} %bitcast.109, s32[512]{0:T(512)S(1)} %multiply_add_fusion.2, f32[512]{0:T(512)S(1)} %broadcast_select_fusion), kind=kOutput, calls=%fused_computation.109 | convolution fusion | flops 12888834048 | bytes 16781312 | tf_op jit(solution)/shard_map/nyz,mn->myz/dot_general | solution.py:61
  590.5 20.1 %fusion.27 = f32[512,128,32]{1,0,2:T(8,128)S(1)} fusion(f32[512,128,32]{1,0,2:T(8,128)S(1)} %fusion.62, f32[32]{0:T(128)S(1)} %multiply_subtract_fusion.2, f32[512,128]{1,0:T(8,128)S(1)} %broadcast_add_fusion, f32[]{:T(128)S(6)} %div.25, pred[512,128]{1,0:T(8,128)(4,1)S(1)} %broadcast_and_fusion, pred[32]{0:T(512)(128)(4,1)S(1)} %fusion.157, ...), kind=kOutput, calls=%fused_computation.67 | convolution fusion | flops 12901416960 | bytes 17109156 | tf_op jit(solution)/shard_map/myz,mn->nyz/dot_general | solution.py:61
  615.5 186.7 %all_to_all.144 = f32[512,128,32]{1,2,0:T(8,128)} all-to-all(f32[512,128,32]{1,2,0:T(8,128)S(1)} %copy.96), channel_id=1, replica_groups=mesh['wide'=4,'narrow'=8] {'wide'}, dimensions={0} | all-to-all | bytes 16777216 | tf_op jit(solution)/shard_map/all_to_all | solution.py:116
  824.6 24.8 %convolution_bitcast_fusion.1 = f32[128,512,32]{0,1,2:T(8,128)S(1)} fusion(f32[128,512,32]{1,0,2:T(8,128)} %all_to_all.115, s32[512]{0:T(512)S(1)} %multiply_add_fusion.2, f32[512]{0:T(512)S(1)} %broadcast_select_fusion), kind=kOutput, calls=%fused_computation.95 | convolution fusion | flops 12888834048 | bytes 16781312 | tf_op jit(solution)/shard_map/xmz,mn->xnz/dot_general | solution.py:61
  854.3 98.0 %all_to_all.145 = f32[128,512,32]{0,2,1:T(8,128)S(1)} all-to-all(f32[128,512,32]{0,2,1:T(8,128)S(1)} %copy.98), channel_id=1, replica_groups=mesh['wide'=4,'narrow'=8] {'narrow'}, dimensions={1} | all-to-all | bytes 16777216 | tf_op jit(solution)/shard_map/all_to_all | solution.py:119
  1008.0 25.2 %multiply_reduce_fusion.1 = (f32[]{:T(128)}, f32[]{:T(128)}, f32[128,64,256]{2,0,1:T(8,128)}) fusion(f32[128,64,256]{2,0,1:T(8,128)S(1)} %fusion.129, f32[128,64,256]{2,0,1:T(8,128)} %fusion.14, f32[128,64,257]{2,0,1:T(8,128)} %fusion.3, f32[128,65,256]{2,0,1:T(8,128)} %fusion.7, f32[129,64,256]{2,0,1:T(8,128)} %fusion.5), kind=kLoop, calls=%fused_computation.65 | loop fusion | flops 20971520 | bytes 75497480 | tf_op jit(solution)/shard_map/reduce_sum | solution.py:149
  1033.1 40.6 %all-reduce.3 = (f32[]{:T(128)}, f32[]{:T(128)}) all-reduce(f32[]{:T(128)} %get-tuple-element.16, f32[]{:T(128)} %get-tuple-element.15), channel_id=1, replica_groups=mesh['wide'=4,'narrow'=8] {'wide','narrow'}, use_global_device_ids=true, to_apply=%region_2.3 | all-reduce | flops 2 | bytes 16 | tf_op jit(solution)/shard_map/psum | solution.py:148
  1108.3 97.8 %all_to_all.146 = f32[128,64,256]{0,1,2:T(8,128)S(1)} all-to-all(f32[128,64,256]{0,1,2:T(8,128)} %copy.102), channel_id=1, replica_groups=mesh['wide'=4,'narrow'=8] {'narrow'}, dimensions={2} | all-to-all | bytes 16777216 | tf_op jit(solution)/shard_map/all_to_all | solution.py:100
  1210.9 29.1 %fusion.46 = f32[128,512,32]{0,1,2:T(8,128)S(1)} fusion(f32[128,512,32]{0,2,1:T(8,128)S(1)} %bitcast.112, s32[512]{0:T(512)S(1)} %multiply_add_fusion.2, f32[512]{0:T(512)S(1)} %broadcast_select_fusion), kind=kOutput, calls=%fused_computation.93 | convolution fusion | flops 12888834048 | bytes 16781312 | tf_op jit(solution)/shard_map/xnz,mn->xmz/dot_general | solution.py:61
  1244.9 186.4 %all_to_all.147 = f32[128,512,32]{0,2,1:T(8,128)} all-to-all(f32[128,512,32]{0,2,1:T(8,128)S(1)} %copy.107), channel_id=1, replica_groups=mesh['wide'=4,'narrow'=8] {'wide'}, dimensions={1} | all-to-all | bytes 16777216 | tf_op jit(solution)/shard_map/all_to_all | solution.py:106
  1441.2 22.5 %fusion.59 = f32[512,128,32]{1,0,2:T(8,128)S(1)} fusion(f32[512,128,32]{1,0,2:T(8,128)} %bitcast.110, s32[512]{0:T(512)S(1)} %multiply_add_fusion.2, f32[512]{0:T(512)S(1)} %broadcast_select_fusion), kind=kOutput, calls=%fused_computation.108 | convolution fusion | flops 12888834048 | bytes 16781312 | tf_op jit(solution)/shard_map/nyz,mn->myz/dot_general | solution.py:61
  1463.7 20.1 %fusion.25 = f32[512,128,32]{1,0,2:T(8,128)S(1)} fusion(f32[512,128,32]{1,0,2:T(8,128)S(1)} %fusion.59, f32[32]{0:T(128)S(1)} %multiply_subtract_fusion.2, f32[512,128]{1,0:T(8,128)S(1)} %broadcast_add_fusion, f32[]{:T(128)S(6)} %div.25, pred[512,128]{1,0:T(8,128)(4,1)S(1)} %broadcast_and_fusion, pred[32]{0:T(512)(128)(4,1)S(1)} %fusion.157, ...), kind=kOutput, calls=%fused_computation.61 | convolution fusion | flops 12901416960 | bytes 17109156 | tf_op jit(solution)/shard_map/myz,mn->nyz/dot_general | solution.py:61
  1488.7 185.9 %all_to_all.148 = f32[512,128,32]{1,2,0:T(8,128)} all-to-all(f32[512,128,32]{1,2,0:T(8,128)S(1)} %copy.111), channel_id=1, replica_groups=mesh['wide'=4,'narrow'=8] {'wide'}, dimensions={0} | all-to-all | bytes 16777216 | tf_op jit(solution)/shard_map/all_to_all | solution.py:116
  1697.0 24.9 %convolution_bitcast_fusion = f32[128,512,32]{0,1,2:T(8,128)S(1)} fusion(f32[128,512,32]{1,0,2:T(8,128)} %all_to_all.131, s32[512]{0:T(512)S(1)} %multiply_add_fusion.2, f32[512]{0:T(512)S(1)} %broadcast_select_fusion), kind=kOutput, calls=%fused_computation.94 | convolution fusion | flops 12888834048 | bytes 16781312 | tf_op jit(solution)/shard_map/xmz,mn->xnz/dot_general | solution.py:61
  1746.7 82.4 %all-to-all-done.7 = f32[128,512,32]{0,2,1:T(8,128)} async-done(((f32[128,512,32]{0,2,1:T(8,128)}), f32[128,512,32]{0,2,1:T(8,128)}, u32[]{:S(2)}, u32[]{:S(2)}) %all-to-all-start.7) | async-done | bytes 8388640 | tf_op jit(solution)/shard_map/all_to_all | solution.py:119
  1833.6 21.2 %multiply_reduce_fusion = (f32[]{:T(128)}, f32[128,64,256]{2,0,1:T(8,128)}) fusion(f32[128,64,256]{2,0,1:T(8,128)} %multiply_subtract_fusion, f32[128,64,256]{0,2,1:T(8,128)S(1)} %bitcast.113, s32[256]{0:T(256)S(1)} %multiply_add_fusion.3, f32[256]{0:T(256)S(1)} %compare_select_fusion), kind=kOutput, calls=%fused_computation.60 | convolution fusion | flops 6447628288 | bytes 25167876 | tf_op jit(solution)/shard_map/xym,mn->xyn/dot_general | solution.py:61
  1854.8 38.1 %psum.23 = f32[]{:T(128)} all-reduce(f32[]{:T(128)} %get-tuple-element.62), channel_id=1, replica_groups=mesh['wide'=4,'narrow'=8] {'wide','narrow'}, use_global_device_ids=true, to_apply=%region_6.7 | all-reduce | flops 1 | bytes 8 | tf_op jit(solution)/shard_map/psum | solution.py:154
  (84 shorter events, 393.6 us)
Async XLA Ops:
  2.4 8.4 copy-start.2
  39.8 9.1 collective-permute-start
  44.7 11.2 copy-start.4
  44.7 8.3 collective-permute-start.1
  53.1 3.4 collective-permute-start.2
  54.6 5.4 collective-permute-start.3
  92.6 6.1 copy-start.1
  221.6 104.3 %all-to-all-start = ((f32[128,64,256]{0,1,2:T(8,128)}), f32[128,64,256]{0,1,2:T(8,128)}, u32[]{:S(2)}, u32[]{:S(2)}) async-start(f32[128,64,256]{0,1,2:T(8,128)} %copy.87), calls=%async_computation | async-start | bytes 16777216 | tf_op jit(solution)/shard_map/all_to_all | solution.py:100
  371.5 5.8 copy-start.3
  371.5 186.6 %all-to-all-start.1 = ((f32[128,512,32]{0,2,1:T(8,128)}), f32[128,512,32]{0,2,1:T(8,128)}, u32[]{:S(2)}, u32[]{:S(2)}) async-start(f32[128,512,32]{0,2,1:T(8,128)} %copy.92), calls=%async_computation.1 | async-start | bytes 16777216 | tf_op jit(solution)/shard_map/all_to_all | solution.py:106
  974.9 33.0 %copy-start = (f32[128,64,256]{2,0,1:T(8,128)}, f32[128,64,256]{2,0,1:T(8,128)S(1)}, u32[]{:S(2)}) copy-start(f32[128,64,256]{2,0,1:T(8,128)S(1)} %fusion.129) | copy-start | bytes 25165828
  975.1 14.2 collective-permute-start.5
  977.2 12.1 collective-permute-start.4
  989.3 11.6 collective-permute-start.6
  990.6 10.3 collective-permute-start.7
  1730.1 99.0 %all-to-all-start.7 = ((f32[128,512,32]{0,2,1:T(8,128)}), f32[128,512,32]{0,2,1:T(8,128)}, u32[]{:S(2)}, u32[]{:S(2)}) async-start(f32[128,512,32]{0,2,1:T(8,128)} %copy.113), calls=%async_computation.7 | async-start | bytes 16777216 | tf_op jit(solution)/shard_map/all_to_all | solution.py:119
where the time goes:
time: 1940 us; the launch traced here: 1930 us
  blocking collectives  834 us (43%)
  waiting for transfers between devices  366 us (19%)
  matrix products  259 us (13%)
  other arithmetic  217 us (11%)
  local copies, waits for them, and re-layouts  210 us (11%)
  starting transfers between devices  37.6 us (2%)
    all_to_all x2, blocking collectives, precondition(): lax.all_to_all(spectral, 'wide', split_axis=0, concat_axis=1, tiled=True)  373 us
    dot_general x12, matrix products, transform(): return jnp.einsum(einsum_form, values, matrix, precision=HIGHEST)  259 us
    all_to_all x1, blocking collectives, precondition(): lax.all_to_all(spectral, 'wide', split_axis=1, concat_axis=0, tiled=True)  186 us
    all_to_all x1, waiting for transfers between devices, precondition(): lax.all_to_all(spectral, 'wide', split_axis=1, concat_axis=0, tiled=True)  179 us
    all_to_all x1, blocking collectives, precondition(): lax.all_to_all(spectral, 'narrow', split_axis=1, concat_axis=2, tiled=True)  98 us
    all_to_all x1, blocking collectives, precondition(): lax.all_to_all(spectral, 'narrow', split_axis=2, concat_axis=1, tiled=True)  97.8 us
    all_to_all x1, waiting for transfers between devices, precondition(): lax.all_to_all(spectral, 'narrow', split_axis=2, concat_axis=1, tiled=True)  94.1 us
    all_to_all x1, waiting for transfers between devices, precondition(): lax.all_to_all(spectral, 'narrow', split_axis=1, concat_axis=2, tiled=True)  82.4 us
  transfers between devices with their start and end apart: 11, of which 6 were waited for; matrix products, arithmetic and copies ran while one was open for 2% of the time, Pallas kernels for 0%

commit v1 on v0

v1 whole, which is shorter than its diff:
```python
import functools

import jax
import jax.numpy as jnp
import ml_dtypes
import numpy as np
from jax import lax
from jax.experimental import pallas as pl
from jax.experimental.pallas import tpu as pltpu
from jax.sharding import PartitionSpec as P

PHASES = 4
F32 = jnp.float32
BF16 = jnp.bfloat16
VMEM_LIMIT = 56 * 1024 * 1024
FORWARD_TERMS = ((0, 0), (0, 1), (1, 0), (1, 1), (0, 2), (2, 0))
INVERSE_TERMS = ((0, 0), (0, 1), (1, 0))


def cosine_table(length):
    m = np.arange(length)[:, None]
    n = np.arange(length)[None, :]
    weight = np.where(m == 0, np.sqrt(1.0 / length), np.sqrt(2.0 / length))
    return weight * np.cos(np.pi * (m * (2 * n + 1) % (4 * length)) / (2.0 * length))


def eigen_values(length):
    return 4.0 * np.sin(np.pi * np.arange(length) / (2.0 * length)) ** 2


def pieces(matrix, count=3):
    rest = np.asarray(matrix, np.float64)
    result = []
    for _ in range(count):
        piece = rest.astype(np.float32).astype(ml_dtypes.bfloat16)
        result.append(piece)
        rest = rest - piece.astype(np.float64)
    return np.stack(result)


def make_tables(size_x, size_y, size_z, wide, narrow):
    length_x = size_x * wide
    group = min(max(256 // size_y, 1), size_x)
    parity = np.concatenate([np.arange(0, size_y, 2), np.arange(1, size_y, 2)])
    strip = cosine_table(size_y)[parity]
    block_y = np.kron(np.eye(group), strip)
    table_z = cosine_table(size_z)
    shift = 4.0 * np.sin(np.pi / (2.0 * length_x)) ** 2
    eig_z = eigen_values(size_z)
    sigma = shift + eigen_values(size_y)[parity][:, None] + eig_z[None, :]
    theta = 2.0 * np.arcsinh(np.sqrt(sigma) / 2.0)
    decay = np.exp(-theta)
    kappa = 1.0 / (2.0 * np.sinh(theta))
    step = np.exp(-theta * size_x)
    total = -np.expm1(-2.0 * wide * size_x * theta)
    powers = np.stack([step**t / total for t in range(2 * wide)])
    border = np.broadcast_to(strip[:, :1], sigma.shape)
    eta = 2.0 * np.arcsinh(
        np.sqrt(shift + eig_z[:, None] + eigen_values(length_x)[None, :]) / 2.0
    )
    fade = np.exp(-eta * size_y)
    half_angle = np.pi * np.arange(1, narrow) / (2.0 * narrow)
    capacity = (np.tanh(eta / 2.0) * -np.expm1(-2.0 * eta * size_y))[None] / (
        (np.expm1(-eta * size_y) ** 2)[None]
        + 4.0 * fade[None] * (np.sin(half_angle) ** 2)[:, None, None]
    )
    part_z = size_z // narrow
    capacity = capacity.reshape(narrow - 1, narrow, part_z, length_x).transpose(1, 0, 2, 3)
    k = np.arange(1, narrow)
    sines = np.sqrt(2.0 / narrow) * np.sin(np.pi * k[:, None] * k[None, :] / narrow)
    table_x = cosine_table(length_x).T.reshape(wide, size_x, length_x)
    f32 = lambda a: np.asarray(a, np.float32)
    return dict(
        group=group,
        z_fwd=pieces(table_z.T),
        z_inv=pieces(table_z, 2),
        y_fwd=pieces(block_y),
        y_inv=pieces(block_y.T, 2),
        decay=f32(decay),
        kappa=f32(kappa),
        powers=f32(powers),
        border=f32(border),
        border_kappa=f32(border * kappa),
        capacity=f32(capacity.reshape(narrow, (narrow - 1) * part_z, length_x)),
        sines=sines,
        table_x=f32(table_x),
    )


def split(values, count):
    result = [values.astype(BF16)]
    rest = values
    for _ in range(count - 1):
        rest = rest - result[-1].astype(F32)
        result.append(rest.astype(BF16))
    return result


def product_right(values, matrix_ref, terms):
    parts = split(values, 1 + max(a for a, _ in terms))
    total = None
    for a, b in reversed(terms):
        term = jnp.dot(parts[a], matrix_ref[b], preferred_element_type=F32)
        total = term if total is None else total + term
    return total


def product_left(matrix_ref, values, terms):
    parts = split(values, 1 + max(a for a, _ in terms))
    total = None
    for a, b in reversed(terms):
        term = jnp.dot(matrix_ref[b], parts[a], preferred_element_type=F32)
        total = term if total is None else total + term
    return total


def lookup(phase, scal, component):
    base = 4 * component
    picked = jnp.where(phase == 2.0, scal[base + 2], scal[base + 3])
    picked = jnp.where(phase == 1.0, scal[base + 1], picked)
    return jnp.where(phase == 0.0, scal[base], picked)


def forward_modes(block, z_ref, y_ref, kappa_ref, decay_ref, modes_ref, ahead_ref, back_ref, power):
    planes, rows, depth = block.shape
    flat = block.reshape(planes * rows, depth)
    flat = product_right(flat, z_ref, FORWARD_TERMS)
    flat = product_left(y_ref, flat, FORWARD_TERMS)
    scaled = flat.reshape(planes, rows, depth) * kappa_ref[...][None]
    modes_ref[...] = scaled
    decay = decay_ref[...]
    ahead, back, weight = (ahead_ref[...], back_ref[...], power[...])
    for j in range(planes):
        ahead = decay * ahead + scaled[j]
        back = back + weight * scaled[j]
        weight = weight * decay
    ahead_ref[...] = ahead
    back_ref[...] = back
    power[...] = weight


def fold(values):
    rows, depth = values.shape
    return jnp.sum(values.reshape(rows // 8, 8, depth), axis=0)


def residual_kernel(
    group, size_x,
    scal, phase_ref, phase_next, field_ref, field_next, x_before, x_after, y_before, y_after,
    z_mat, y_mat, kappa_ref, decay_ref,
    residual_ref, modes_ref, fx_ref, fy_ref, fz_ref, fx_low, fy_low, ahead_ref, back_ref,
    flux_low, power,
):
    step = pl.program_id(0)
    rows, depth = flux_low.shape
    gx, gy, gz = scal[12], scal[13], scal[14]
    flag_xb, flag_xa, flag_yb, flag_ya = scal[15], scal[16], scal[17], scal[18]
    row = lax.broadcasted_iota(jnp.int32, (rows, depth), 0)
    lane = lax.broadcasted_iota(jnp.int32, (rows, depth), 1)

    @pl.when(step == 0)
    def _():
        face = flag_xb / (lookup(x_before[0], scal, 0) + lookup(phase_ref[0].astype(F32), scal, 0))
        fx_low[...] = face
        flux_low[...] = face * (field_ref[0] - x_before[1] + gx)
        ahead_ref[...] = jnp.zeros_like(ahead_ref)
        back_ref[...] = jnp.zeros_like(back_ref)
        power[...] = jnp.ones_like(power)

    last = step == pl.num_programs(0) - 1
    end_phase = jnp.where(last, x_after[0], phase_next[0].astype(F32))
    end_field = jnp.where(last, x_after[1], field_next[0])
    flag_end = jnp.where(last, flag_xa, 1.0)
    flux_x_low = flux_low[...]
    hx = lookup(phase_ref[0].astype(F32), scal, 0)
    for j in range(group):
        x = step * group + j
        phase = phase_ref[j].astype(F32)
        field = field_ref[j]
        if j + 1 < group:
            hx_next = lookup(phase_ref[j + 1].astype(F32), scal, 0)
            field_up = field_ref[j + 1]
            fx = 1.0 / (hx + hx_next)
        else:
            hx_next = lookup(end_phase, scal, 0)
            field_up = end_field
            fx = flag_end / (hx + hx_next)
        flux_x = fx * (field_up - field + gx)
        total = flux_x - flux_x_low
        flux_x_low, hx = flux_x, hx_next
        fx_ref[j] = fx

        hy = lookup(phase, scal, 1)
        hy_up = jnp.where(
            row == rows - 1,
            lookup(y_after[0, pl.ds(x, 1), :], scal, 1),
            pltpu.roll(hy, rows - 1, 0),
        )
        fy = jnp.where(row == rows - 1, flag_ya, 1.0) / (hy + hy_up)
        v_up = jnp.where(row == rows - 1, y_after[1, pl.ds(x, 1), :], pltpu.roll(field, rows - 1, 0))
        flux_y = fy * (v_up - field + gy)
        face = flag_yb / (lookup(y_before[0, pl.ds(x, 1), :], scal, 1) + hy[0:1])
        low = face * (field[0:1] - y_before[1, pl.ds(x, 1), :] + gy)
        total = total + (flux_y - jnp.where(row == 0, low, pltpu.roll(flux_y, 1, 0)))
        fy_ref[j] = fy
        fy_low[pl.ds(x, 1), :] = face

        hz = lookup(phase, scal, 2)
        fz = jnp.where(lane == depth - 1, 0.0, 1.0 / (hz + pltpu.roll(hz, depth - 1, 1)))
        flux_z = fz * (pltpu.roll(field, depth - 1, 1) - field + gz)
        total = total + (flux_z - pltpu.roll(flux_z, 1, 1))
        fz_ref[j] = fz
        residual_ref[j] = total
    flux_low[...] = flux_x_low
    forward_modes(
        residual_ref[...], z_mat, y_mat, kappa_ref, decay_ref, modes_ref, ahead_ref, back_ref, power
    )


def image_kernel(
    group, size_x,
    field_ref, field_next, residual_ref, fx_ref, fy_ref, fz_ref, fx_low, fy_low,
    x_before, x_after, y_before, y_after, z_mat, y_mat, kappa_ref, decay_ref,
    image_ref, modes_ref, ahead_ref, back_ref, sums_ref,
    flux_low, power,
):
    step = pl.program_id(0)
    rows, depth = flux_low.shape
    row = lax.broadcasted_iota(jnp.int32, (rows, depth), 0)

    @pl.when(step == 0)
    def _():
        flux_low[...] = fx_low[...] * (field_ref[0] - x_before[...])
        ahead_ref[...] = jnp.zeros_like(ahead_ref)
        back_ref[...] = jnp.zeros_like(back_ref)
        power[...] = jnp.ones_like(power)
        sums_ref[...] = jnp.zeros_like(sums_ref)

    last = step == pl.num_programs(0) - 1
    end_field = jnp.where(last, x_after[...], field_next[0])
    flux_x_low = flux_low[...]
    sums = [sums_ref[i] for i in range(5)]
    for j in range(group):
        x = step * group + j
        field = field_ref[j]
        field_up = field_ref[j + 1] if j + 1 < group else end_field
        flux_x = fx_ref[j] * (field_up - field)
        total = flux_x_low - flux_x
        flux_x_low = flux_x
        v_up = jnp.where(row == rows - 1, y_after[pl.ds(x, 1), :], pltpu.roll(field, rows - 1, 0))
        flux_y = fy_ref[j] * (v_up - field)
        low = fy_low[pl.ds(x, 1), :] * (field[0:1] - y_before[pl.ds(x, 1), :])
        total = total + (jnp.where(row == 0, low, pltpu.roll(flux_y, 1, 0)) - flux_y)
        flux_z = fz_ref[j] * (pltpu.roll(field, depth - 1, 1) - field)
        total = total + (pltpu.roll(flux_z, 1, 1) - flux_z)
        image_ref[j] = total
        res = residual_ref[j]
        for i, term in enumerate((res * field, res, field * total, total, field)):
            sums[i] = sums[i] + fold(term)
    for i in range(5):
        sums_ref[i] = sums[i]
    flux_low[...] = flux_x_low
    forward_modes(
        image_ref[...], z_mat, y_mat, kappa_ref, decay_ref, modes_ref, ahead_ref, back_ref, power
    )


def incoming(wide, mine, ends_ref, powers_ref, towards):
    total = None
    for block in range(2 * wide):
        mirrored = block >= wide
        source = 2 * wide - 1 - block if mirrored else block
        if towards > 0:
            value = ends_ref[source, 1 if mirrored else 0]
            distance = mine - 1 - block
        else:
            value = ends_ref[source, 0 if mirrored else 1]
            distance = block - 1 - mine
        distance = lax.rem(distance + 4 * wide, 2 * wide)
        term = powers_ref[distance] * value
        total = term if total is None else total + term
    return total


def border_kernel(
    wide, narrow, planes,
    index, modes_ref, ends_ref, powers_ref, decay_ref, border_ref,
    out_ref,
    run, kept, rows_ref,
):
    phase, step = pl.program_id(0), pl.program_id(1)
    blocks = pl.num_programs(1)
    decay = decay_ref[...]
    half = decay.shape[0] // 2

    @pl.when((phase == 0) & (step == 0))
    def _():
        run[...] = incoming(wide, index[0], ends_ref, powers_ref, 1)

    @pl.when(phase == 0)
    def _():
        value = run[...]
        for j in range(planes):
            value = modes_ref[j] + decay * value
            kept[step * planes + j] = value
        run[...] = value

    @pl.when((phase == 1) & (step == 0))
    def _():
        run[...] = incoming(wide, index[0], ends_ref, powers_ref, -1)

    @pl.when(phase == 1)
    def _():
        value = run[...]
        border = border_ref[...]
        first = (blocks - 1 - step) * planes
        for j in reversed(range(planes)):
            passed = decay * value
            mode = (kept[first + j] + passed) * border
            value = modes_ref[j] + passed
            rows_ref[0, pl.ds(first + j, 1), :] = jnp.sum(mode[:half], axis=0, keepdims=True)
            rows_ref[1, pl.ds(first + j, 1), :] = jnp.sum(mode[half:], axis=0, keepdims=True)
        run[...] = value

    @pl.when((phase == 1) & (step == blocks - 1))
    def _():
        part = out_ref.shape[2]
        for side in range(2):
            turned = rows_ref[side].T
            for j in range(narrow):
                out_ref[j, side] = turned[j * part : (j + 1) * part]


def capacity_kernel(wide, narrow, sines, index, jump_ref, table_ref, capacity_ref, out_ref, scratch):
    faces, part, _ = jump_ref.shape[1:]
    mode = None
    for block in range(wide):
        jumps = [jump_ref[block, k] for k in range(faces)]
        for k in range(faces):
            acc = None
            for i in range(faces):
                term = jumps[i] * float(sines[k, i])
                acc = term if acc is None else acc + term
            scratch[pl.ds(k * part, part), :] = acc
        term = jnp.dot(
            scratch[...], table_ref[block], preferred_element_type=F32, precision=lax.Precision.HIGHEST
        )
        mode = term if mode is None else mode + term
    mode = mode * capacity_ref[0]
    scratch[...] = lax.dot_general(
        mode, table_ref[index[0]], (((1,), (1,)), ((), ())),
        preferred_element_type=F32, precision=lax.Precision.HIGHEST,
    )
    solved = []
    for k in range(faces):
        acc = None
        for i in range(faces):
            term = scratch[pl.ds(i * part, part), :] * float(sines[k, i])
            acc = term if acc is None else acc + term
        solved.append(acc)
    for strip in range(narrow):
        if strip == 0:
            even, odd = solved[0], -solved[0]
        elif strip == narrow - 1:
            even, odd = -solved[-1], -solved[-1]
        else:
            even = solved[strip] - solved[strip - 1]
            odd = -(solved[strip] + solved[strip - 1])
        out_ref[strip, 0] = even
        out_ref[strip, 1] = odd


def ends_kernel(narrow, face_ref, ends_ref, decay_ref, scale_ref, out_ref, rows_ref, turned):
    part = face_ref.shape[2]
    for side in range(2):
        for j in range(narrow):
            turned[pl.ds(j * part, part), :] = face_ref[j, side]
        rows_ref[side] = turned[...].T
    size_x = rows_ref.shape[1]
    half = decay_ref.shape[0] // 2
    for side in range(2):
        decay = decay_ref[pl.ds(side * half, half), :]

        def body(x, carry):
            ahead, back = carry
            ahead = decay * ahead + rows_ref[side, pl.ds(x, 1), :]
            back = decay * back + rows_ref[side, pl.ds(size_x - 1 - x, 1), :]
            return ahead, back

        zero = jnp.zeros_like(decay)
        ahead, back = lax.fori_loop(0, size_x, body, (zero, zero), unroll=8)
        scale = scale_ref[pl.ds(side * half, half), :]
        out_ref[0, pl.ds(side * half, half), :] = ends_ref[0, pl.ds(side * half, half), :] + scale * ahead
        out_ref[1, pl.ds(side * half, half), :] = ends_ref[1, pl.ds(side * half, half), :] + scale * back


def inverse_kernel(
    wide, planes, dotted,
    index, modes_ref, ends_ref, powers_ref, decay_ref, scale_ref, rows_ref, y_mat, z_mat, *rest,
):
    if dotted:
        residual_ref, image_ref, out_ref, sums_ref, run, kept, fixed = rest
    else:
        out_ref, first_ref, last_ref, run, kept, fixed = rest
    phase, step = pl.program_id(0), pl.program_id(1)
    blocks = pl.num_programs(1)
    decay = decay_ref[...]
    rows, depth = decay.shape
    half = rows // 2

    @pl.when((phase == 0) & (step == 0))
    def _():
        run[...] = incoming(wide, index[0], ends_ref, powers_ref, 1)

    @pl.when(phase == 0)
    def _():
        value = run[...]
        scale = scale_ref[...]
        for j in range(planes):
            x = step * planes + j
            face = jnp.concatenate(
                [
                    jnp.broadcast_to(rows_ref[0, pl.ds(x, 1), :], (half, depth)),
                    jnp.broadcast_to(rows_ref[1, pl.ds(x, 1), :], (half, depth)),
                ],
                axis=0,
            )
            mode = modes_ref[j] + scale * face
            value = mode + decay * value
            fixed[x] = mode
            kept[x] = value
        run[...] = value

    @pl.when((phase == 1) & (step == 0))
    def _():
        run[...] = incoming(wide, index[0], ends_ref, powers_ref, -1)
        if dotted:
            sums_ref[...] = jnp.zeros_like(sums_ref)

    @pl.when(phase == 1)
    def _():
        value = run[...]
        first = (blocks - 1 - step) * planes
        for j in reversed(range(planes)):
            passed = decay * value
            value = fixed[first + j] + passed
            kept[first + j] = kept[first + j] + passed
        run[...] = value
        flat = kept[pl.ds(first, planes)].reshape(planes * rows, depth)
        flat = product_left(y_mat, flat, INVERSE_TERMS)
        flat = product_right(flat, z_mat, INVERSE_TERMS)
        block = flat.reshape(planes, rows, depth)
        out_ref[...] = block
        if dotted:
            sums = [sums_ref[i] for i in range(3)]
            for j in range(planes):
                for i, term in enumerate((residual_ref[j] * block[j], image_ref[j] * block[j], block[j])):
                    sums[i] = sums[i] + fold(term)
            for i in range(3):
                sums_ref[i] = sums[i]
        else:
            for j in range(planes):
                first_ref[pl.ds(first + j, 1), :] = block[j, 0:1]
                last_ref[pl.ds(first + j, 1), :] = block[j, rows - 1 : rows]


def whole(shape, single=False):
    mode = dict(pipeline_mode=pl.Buffered(1)) if single else {}
    return pl.BlockSpec(shape, lambda *_: (0,) * len(shape), **mode)


def shape_of(*dims):
    return jax.ShapeDtypeStruct(dims, F32)


def params(dims):
    return pltpu.CompilerParams(dimension_semantics=("arbitrary",) * dims, vmem_limit_bytes=VMEM_LIMIT)


def neighbours(axis):
    devices = lax.axis_size(axis)
    up = [(i, i + 1) for i in range(devices - 1)]
    return up, [(j, i) for i, j in up]


def exchange(first, last, axis):
    up, down = neighbours(axis)
    return lax.ppermute(last, axis, up), lax.ppermute(first, axis, down)


def solve(modes, ends, tab, index, kind, extra=()):
    size_x, size_y, size_z = modes.shape
    wide, narrow = lax.axis_size("wide"), lax.axis_size("narrow")
    group = tab["group"]
    blocks = size_x // group
    part = size_z // narrow
    plane = (size_y, size_z)
    wide_at = index[:1]
    sweep = lambda p, i, *_: (jnp.where(p == 0, i, blocks - 1 - i), 0, 0)
    ends_all = lax.all_gather(ends, "wide", axis=0)
    borders = pl.pallas_call(
        functools.partial(border_kernel, wide, narrow, group),
        out_shape=shape_of(narrow, 2, part, size_x),
        grid_spec=pltpu.PrefetchScalarGridSpec(
            num_scalar_prefetch=1,
            grid=(2, blocks),
            in_specs=[
                pl.BlockSpec((group,) + plane, sweep),
                whole((wide, 2) + plane),
                whole((2 * wide,) + plane),
                whole(plane),
                whole(plane),
            ],
            out_specs=whole((narrow, 2, part, size_x)),
            scratch_shapes=[
                pltpu.VMEM(plane, F32),
                pltpu.VMEM((size_x,) + plane, F32),
                pltpu.VMEM((2, size_x, size_z), F32),
            ],
        ),
        compiler_params=params(2),
        name="strip_borders",
    )(wide_at, modes, ends_all, tab["powers"], tab["decay"], tab["border"])
    strips = lax.all_to_all(borders, "narrow", split_axis=0, concat_axis=0, tiled=True)
    jumps = strips[1:, 0] + strips[1:, 1] - strips[:-1, 0] + strips[:-1, 1]
    jumps = lax.all_gather(jumps, "wide", axis=0)
    faces = narrow - 1
    length_x = wide * size_x
    solved = pl.pallas_call(
        functools.partial(capacity_kernel, wide, narrow, tab["sines"]),
        out_shape=shape_of(narrow, 2, part, size_x),
        grid_spec=pltpu.PrefetchScalarGridSpec(
            num_scalar_prefetch=1,
            grid=(1,),
            in_specs=[
                whole((wide, faces, part, size_x)),
                whole((wide, size_x, length_x)),
                pl.BlockSpec((1, faces * part, length_x), lambda i, idx: (idx[1], 0, 0)),
            ],
            out_specs=whole((narrow, 2, part, size_x)),
            scratch_shapes=[pltpu.VMEM((faces * part, size_x), F32)],
        ),
        compiler_params=params(1),
        name="strip_faces",
    )(index, jumps, tab["table_x"], tab["capacity"])
    faces_mine = lax.all_to_all(solved, "narrow", split_axis=0, concat_axis=0, tiled=True)
    ends_fixed, rows = pl.pallas_call(
        functools.partial(ends_kernel, narrow),
        out_shape=(shape_of(2, *plane), shape_of(2, size_x, size_z)),
        in_specs=[pl.BlockSpec(memory_space=pltpu.VMEM)] * 4,
        out_specs=(pl.BlockSpec(memory_space=pltpu.VMEM),) * 2,
        scratch_shapes=[pltpu.VMEM((size_z, size_x), F32)],
        compiler_params=pltpu.CompilerParams(vmem_limit_bytes=VMEM_LIMIT),
        name="block_ends",
    )(faces_mine, ends, tab["decay"], tab["border_kappa"])
    ends_all = lax.all_gather(ends_fixed, "wide", axis=0)
    dotted = bool(extra)
    back = lambda p, i, *_: (jnp.where(p == 0, blocks - 1, blocks - 1 - i), 0, 0)
    ahead = lambda p, i, *_: (jnp.where(p == 0, i, blocks - 1), 0, 0)
    block = (group,) + plane
    if dotted:
        out_shape = (shape_of(size_x, *plane), shape_of(3, 8, size_z))
        out_specs = (pl.BlockSpec(block, back), whole((3, 8, size_z)))
    else:
        out_shape = (shape_of(size_x, *plane),) + (shape_of(size_x, size_z),) * 2
        out_specs = (pl.BlockSpec(block, back),) + (whole((size_x, size_z)),) * 2
    return pl.pallas_call(
        functools.partial(inverse_kernel, wide, group, dotted),
        out_shape=out_shape,
        grid_spec=pltpu.PrefetchScalarGridSpec(
            num_scalar_prefetch=1,
            grid=(2, blocks),
            in_specs=[
                pl.BlockSpec(block, ahead),
                whole((wide, 2) + plane),
                whole((2 * wide,) + plane),
                whole(plane),
                whole(plane),
                whole((2, size_x, size_z)),
                whole(tab["y_inv"].shape),
                whole(tab["z_inv"].shape),
            ]
            + [pl.BlockSpec(block, back)] * len(extra),
            out_specs=out_specs,
            scratch_shapes=[
                pltpu.VMEM(plane, F32),
                pltpu.VMEM((size_x,) + plane, F32),
                pltpu.VMEM((size_x,) + plane, F32),
            ],
        ),
        compiler_params=params(2),
        name="inverse_modes",
    )(
        wide_at, modes, ends_all, tab["powers"], tab["decay"], tab["border_kappa"], rows,
        tab["y_inv"], tab["z_inv"], *extra,
    )


def on_device(phase_ids, conduct_table, gradient, start_field):
    size_x, size_y, size_z = start_field.shape
    wide, narrow = lax.axis_size("wide"), lax.axis_size("narrow")
    tab = make_tables(size_x, size_y, size_z, wide, narrow)
    tab = {k: jnp.asarray(v) if isinstance(v, np.ndarray) and k != "sines" else v for k, v in tab.items()}
    group = tab["group"]
    blocks = size_x // group
    plane = (size_y, size_z)
    block = (group,) + plane
    wide_at, narrow_at = lax.axis_index("wide"), lax.axis_index("narrow")
    index = jnp.stack([wide_at, narrow_at]).astype(jnp.int32)
    flags = jnp.stack([wide_at > 0, wide_at < wide - 1, narrow_at > 0, narrow_at < narrow - 1])
    scal = jnp.concatenate([(0.5 / conduct_table).T.reshape(-1), gradient, flags.astype(F32)])
    kappa = tab["kappa"] / jnp.mean(conduct_table)

    edge = lambda dim, at: jnp.stack(
        [lax.index_in_dim(phase_ids, at, dim, False).astype(F32), lax.index_in_dim(start_field, at, dim, False)]
    )
    x_before, x_after = exchange(edge(0, 0), edge(0, size_x - 1), "wide")
    y_before, y_after = exchange(edge(1, 0), edge(1, size_y - 1), "narrow")

    main = pl.BlockSpec(block, lambda i: (i, 0, 0))
    following = pl.BlockSpec((1,) + plane, lambda i: (jnp.minimum((i + 1) * group, size_x - 1), 0, 0))
    field_shape = shape_of(size_x, *plane)
    matrices = [whole(tab["z_fwd"].shape), whole(tab["y_fwd"].shape), whole(plane), whole(plane)]
    carried = [pltpu.VMEM(plane, F32), pltpu.VMEM(plane, F32)]
    residual, modes, fx, fy, fz, fx_low, fy_low, ahead, back = pl.pallas_call(
        functools.partial(residual_kernel, group, size_x),
        grid=(blocks,),
        out_shape=(field_shape,) * 5 + (shape_of(*plane), shape_of(size_x, size_z)) + (shape_of(*plane),) * 2,
        in_specs=[pl.BlockSpec(memory_space=pltpu.SMEM), main, following, main, following]
        + [whole((2,) + plane)] * 2
        + [whole((2, size_x, size_z))] * 2
        + matrices,
        out_specs=(main,) * 5 + (whole(plane), whole((size_x, size_z))) + (whole(plane),) * 2,
        scratch_shapes=carried,
        compiler_params=params(1),
        name="residual_modes",
    )(
        scal, phase_ids, phase_ids, start_field, start_field, x_before, x_after, y_before, y_after,
        tab["z_fwd"], tab["y_fwd"], kappa, tab["decay"],
    )
    along, row_first, row_last = solve(modes, jnp.stack([ahead, back]), tab, index, 0)

    xb, xa = exchange(along[0], along[size_x - 1], "wide")
    yb, ya = exchange(row_first, row_last, "narrow")
    image, modes, ahead, back, sums = pl.pallas_call(
        functools.partial(image_kernel, group, size_x),
        grid=(blocks,),
        out_shape=(field_shape,) * 2 + (shape_of(*plane),) * 2 + (shape_of(5, 8, size_z),),
        in_specs=[main, following] + [main] * 4
        + [whole(plane), whole((size_x, size_z))]
        + [whole(plane)] * 2
        + [whole((size_x, size_z))] * 2
        + matrices,
        out_specs=(main,) * 2 + (whole(plane),) * 2 + (whole((5, 8, size_z)),),
        scratch_shapes=carried,
        compiler_params=params(1),
        name="image_modes",
    )(
        along, along, residual, fx, fy, fz, fx_low, fy_low, xb, xa, yb, ya,
        tab["z_fwd"], tab["y_fwd"], kappa, tab["decay"],
    )
    turned, sums_late = solve(modes, jnp.stack([ahead, back]), tab, index, 1, (residual, image))

    sums = jnp.concatenate([jnp.sum(sums, axis=(1, 2)), jnp.sum(sums_late, axis=(1, 2))])
    sums = lax.psum(lax.psum(sums, "narrow"), "wide")
    res_along, res_one, along_image, image_one, along_one, res_turned, image_turned, turned_one = [
        sums[i] for i in range(8)
    ]
    voxels = float(size_x * wide * size_y * narrow * size_z)
    mean_along = along_one / voxels
    mean_turned = turned_one / voxels
    rz_now = res_along - mean_along * res_one
    curvature = along_image - mean_along * image_one
    alpha = rz_now / curvature
    cross = res_turned - mean_turned * res_one
    square = image_turned - mean_turned * image_one
    rz_next = rz_now - alpha * (cross + curvature) + alpha * (alpha * square)
    beta = rz_next / rz_now
    direction = along - mean_along
    return (
        start_field + alpha * direction,
        residual - alpha * image,
        direction * (1.0 + beta) - alpha * (turned - mean_turned),
    )


def solution(mesh):
    placed = (P("wide", "narrow", None), P(), P(), P("wide", "narrow", None))
    return jax.shard_map(
        on_device,
        mesh=mesh,
        in_specs=placed,
        out_specs=(P("wide", "narrow", None),) * 3,
        check_vma=False,
    )
```

time: 1940 us -> 522 us (0.27)
  blocking collectives: 834 us -> 147 us
  waiting for transfers between devices: 366 us -> 15 us
  Pallas kernels: 0 us -> 276 us
  matrix products: 259 us -> 0 us
  local copies, waits for them, and re-layouts: 210 us -> 8.95 us
  other arithmetic: 217 us -> 34.9 us
    all_to_all x5 -> x2, blocking collectives: 755 us -> 23.5 us  [the longest x1 12.5 us: solve(): lax.all_to_all(borders, 'narrow', split_axis=0, concat_axis=0, tiled=True)]
    all_to_all x3 -> x2, waiting for transfers between devices: 356 us -> 13.1 us  [the longest x1 6.73 us: solve(): lax.all_to_all(solved, 'narrow', split_axis=0, concat_axis=0, tiled=True)]
    pallas_call x0 -> x10, Pallas kernels: none -> 276 us  [the longest x2 90.6 us: solve(): pl.pallas_call(functools.partial(inverse_kernel, wide, group, dotted), ou...]
    dot_general x12 -> x0, matrix products: 259 us -> none  [transform(): return jnp.einsum(einsum_form, values, matrix, precision=HIGHEST)]
    all_gather x0 -> x6, blocking collectives: none -> 101 us  [the longest x2 35.1 us: solve(): ends_all = lax.all_gather(ends, 'wide', axis=0)]
    all_to_all x10 -> x0, local copies, waits for them, and re-layouts: 86.4 us -> none  [the longest x4 44.9 us: precondition(): lax.all_to_all(spectral, 'wide', split_axis=0, concat_axis=1, tiled=True)]
    mul x6 -> x0, other arithmetic: 85.3 us -> none  [the longest x2 32.8 us: apply_padded(): flux_z = faces[2] * (inner_z[:, :, 1:] - inner_z[:, :, :-1])]
    psum x2, blocking collectives: 78.8 us -> 23 us  [on_device(): sums = lax.psum(lax.psum(sums, 'narrow'), 'wide')]
  transfers between devices with their start and end apart: 11 -> 10, of which waited for: 6 -> 4; matrix products, arithmetic and copies ran while one was open for 2% -> 2% of each run, Pallas kernels for 0% -> 0%
where the time goes in v1:
time: 522 us; the launch traced here: 517 us
  Pallas kernels  276 us (53%)
  blocking collectives  147 us (28%)
  other arithmetic  34.9 us (7%)
  starting transfers between devices  26.7 us (5%)
  waiting for transfers between devices  15 us (3%)
  local copies, waits for them, and re-layouts  8.95 us (2%)
  between operations  8 us (2%)
    pallas_call x2, Pallas kernels, solve(): pl.pallas_call(functools.partial(inverse_kernel, wide, group, dotted), ou...  90.6 us
    pallas_call x2, Pallas kernels, solve(): pl.pallas_call(functools.partial(border_kernel, wide, narrow, group), out...  69.7 us
    pallas_call x1, Pallas kernels, on_device(): pl.pallas_call(functools.partial(residual_kernel, group, size_x), grid=(b...  51.8 us
    pallas_call x1, Pallas kernels, on_device(): pl.pallas_call(functools.partial(image_kernel, group, size_x), grid=(bloc...  46.8 us
    all_gather x2, blocking collectives, solve(): ends_all = lax.all_gather(ends, 'wide', axis=0)  35.1 us
    all_gather x2, blocking collectives, solve(): ends_all = lax.all_gather(ends_fixed, 'wide', axis=0)  34.1 us
    all_gather x2, blocking collectives, solve(): jumps = lax.all_gather(jumps, 'wide', axis=0)  31.8 us
    psum x2, blocking collectives, on_device(): sums = lax.psum(lax.psum(sums, 'narrow'), 'wide')  23 us
  transfers between devices with their start and end apart: 10, of which 4 were waited for; matrix products, arithmetic and copies ran while one was open for 2% of the time, Pallas kernels for 0%

profile of v1, /device:TPU:0, one launch (start us, length us, event | category | flops | bytes accessed | tf_op | source)
XLA Modules:
  0.0 516.9 jit_solution(12284036990919059576)
XLA Ops:
  2.4 4.9 collective-permute-start
  21.5 51.8 %residual_modes.1 = (f32[128,64,256]{2,1,0:T(8,128)}, f32[128,64,256]{2,1,0:T(8,128)}, f32[128,64,256]{2,1,0:T(8,128)}, f32[128,64,256]{2,1,0:T(8,128)}, f32[128...) custom-call(f32[19]{0:T(128)} %pad_maximum_fusion.6.scal, ...), custom_call_target="tpu_custom_call" | custom-call | tf_op jit(solution)/shard_map/residual_modes/pallas_call | solution.py:625
  74.1 18.0 %all-gather = f32[8,64,256]{2,1,0:T(8,128)} all-gather(f32[2,64,256]{2,1,0:T(8,128)S(1)} %pad_maximum_fusion.4.ends_ref), channel_id=2, replica_groups=mesh['wide'=4,'narrow'=8] {'wide'}, dimensions={0}, use_global_device_ids=true | all-gather | bytes 655360 | tf_op jit(solution)/shard_map/all_gather | solution.py:500
  92.1 34.8 %strip_borders.2 = f32[8,2,32,128]{3,2,1,0:T(8,128)} custom-call(s32[1]{0:T(128)} %bitcast.index, f32[128,64,256]{2,1,0:T(8,128)} %get-tuple-element.26.modes_ref, f32[4,2,64,256]{3,2,1,0:T(8,128)} %bitcast.42, f32[8,64,256]{2,1,0:T(8,128)} %constant.57.clone.powers_ref, f32[64,256]{1,0:T(8,128)} %constant.55.clone.decay_ref, ...), custom_call_target="tpu_custom_call" | custom-call | tf_op jit(solution)/shard_map/strip_borders/pallas_call | solution.py:501
  127.0 5.9 %all-to-all-start = ((f32[8,2,32,128]{3,2,1,0:T(8,128)}), f32[8,2,32,128]{3,2,1,0:T(8,128)S(1)}, u32[]{:S(2)}, u32[]{:S(2)}) async-start(f32[8,2,32,128]{3,2,1,0:T(8,128)} %strip_borders.2), calls=%async_computation | async-start | bytes 524288 | tf_op jit(solution)/shard_map/all_to_all | solution.py:524
  133.4 6.3 %all-to-all-done = f32[8,2,32,128]{3,2,1,0:T(8,128)S(1)} async-done(((f32[8,2,32,128]{3,2,1,0:T(8,128)}), f32[8,2,32,128]{3,2,1,0:T(8,128)S(1)}, u32[]{:S(2)}, u32[]{:S(2)}) %all-to-all-start) | async-done | bytes 262176 | tf_op jit(solution)/shard_map/all_to_all | solution.py:524
  139.8 16.0 %all-gather.1 = f32[28,1,32,128]{3,2,1,0:T(8,128)} all-gather(f32[7,1,32,128]{3,2,1,0:T(8,128)S(1)} %slice_add_fusion.2), channel_id=3, replica_groups=mesh['wide'=4,'narrow'=8] {'wide'}, dimensions={0}, use_global_device_ids=true | all-gather | bytes 573440 | tf_op jit(solution)/shard_map/all_gather | solution.py:526
  155.8 5.3 %strip_faces.2 = f32[8,2,32,128]{3,2,1,0:T(8,128)} custom-call(s32[2]{0:T(128)} %pad_add_fusion.index, f32[4,7,32,128]{3,2,1,0:T(8,128)} %bitcast.45, f32[4,128,512]{2,1,0:T(8,128)} %constant.61.clone.table_ref, f32[8,224,512]{2,1,0:T(8,128)} %constant.60.clone.capacity_ref), custom_call_target="tpu_custom_call" | custom-call | tf_op jit(solution)/shard_map/strip_faces/pallas_call | solution.py:529
  161.2 11.0 %all_to_all.20.face_ref = f32[8,2,32,128]{3,2,1,0:T(8,128)} all-to-all(f32[8,2,32,128]{3,2,1,0:T(8,128)} %strip_faces.2), channel_id=1, replica_groups=mesh['wide'=4,'narrow'=8] {'narrow'}, dimensions={0} | all-to-all | bytes 524288 | tf_op jit(solution)/shard_map/all_to_all | solution.py:546
  175.3 17.8 %all-gather.2 = f32[8,64,256]{2,1,0:T(8,128)} all-gather(f32[2,64,256]{2,1,0:T(8,128)} %get-tuple-element.29), channel_id=4, replica_groups=mesh['wide'=4,'narrow'=8] {'wide'}, dimensions={0}, use_global_device_ids=true | all-gather | bytes 655360 | tf_op jit(solution)/shard_map/all_gather | solution.py:556
  193.1 42.3 %inverse_modes.2 = (f32[128,64,256]{2,1,0:T(8,128)}, f32[128,256]{1,0:T(8,128)}, f32[128,256]{1,0:T(8,128)}) custom-call(s32[1]{0:T(128)} %bitcast.index, f32[128,64,256]{2,1,0:T(8,128)} %get-tuple-element.26.modes_ref, f32[4,2,64,256]{3,2,1,0:T(8,128)} %bitcast.43, f32[8,64,256]{2,1,0:T(8,128)} %constant.57.clone.powers_ref, ...), custom_call_target="tpu_custom_call" | custom-call | tf_op jit(solution)/shard_map/inverse_modes/pallas_call | solution.py:567
  247.3 46.8 %image_modes.1 = (f32[128,64,256]{2,1,0:T(8,128)}, f32[128,64,256]{2,1,0:T(8,128)}, f32[64,256]{1,0:T(8,128)}, f32[64,256]{1,0:T(8,128)}, f32[5,8,256]{2,1,0:T(8,128)}) custom-call(f32[128,64,256]{2,1,0:T(8,128)} %get-tuple-element.31.field_ref.field_next, f32[128,64,256]{2,1,0:T(8,128)} %get-tuple-element.31.field_ref.field_next, ...), custom_call_target="tpu_custom_call" | custom-call | tf_op jit(solution)/shard_map/image_modes/pallas_call | solution.py:645
  295.1 17.1 %all-gather.3 = f32[8,64,256]{2,1,0:T(8,128)} all-gather(f32[2,64,256]{2,1,0:T(8,128)S(1)} %pad_maximum_fusion.5.ends_ref), channel_id=5, replica_groups=mesh['wide'=4,'narrow'=8] {'wide'}, dimensions={0}, use_global_device_ids=true | all-gather | bytes 655360 | tf_op jit(solution)/shard_map/all_gather | solution.py:500
  312.2 34.9 %strip_borders.3 = f32[8,2,32,128]{3,2,1,0:T(8,128)} custom-call(s32[1]{0:T(128)} %bitcast.index, f32[128,64,256]{2,1,0:T(8,128)} %get-tuple-element.41.modes_ref, f32[4,2,64,256]{3,2,1,0:T(8,128)} %bitcast.41, f32[8,64,256]{2,1,0:T(8,128)} %constant.57.clone.powers_ref, f32[64,256]{1,0:T(8,128)} %constant.55.clone.decay_ref, ...), custom_call_target="tpu_custom_call" | custom-call | tf_op jit(solution)/shard_map/strip_borders/pallas_call | solution.py:501
  347.1 12.5 %all_to_all.21 = f32[8,2,32,128]{3,2,1,0:T(8,128)S(1)} all-to-all(f32[8,2,32,128]{3,2,1,0:T(8,128)} %strip_borders.3), channel_id=1, replica_groups=mesh['wide'=4,'narrow'=8] {'narrow'}, dimensions={0} | all-to-all | bytes 524288 | tf_op jit(solution)/shard_map/all_to_all | solution.py:524
  359.6 15.7 %all-gather.4 = f32[28,1,32,128]{3,2,1,0:T(8,128)} all-gather(f32[7,1,32,128]{3,2,1,0:T(8,128)S(1)} %slice_add_fusion), channel_id=6, replica_groups=mesh['wide'=4,'narrow'=8] {'wide'}, dimensions={0}, use_global_device_ids=true | all-gather | bytes 573440 | tf_op jit(solution)/shard_map/all_gather | solution.py:526
  375.3 5.3 %strip_faces.3 = f32[8,2,32,128]{3,2,1,0:T(8,128)} custom-call(s32[2]{0:T(128)} %pad_add_fusion.index, f32[4,7,32,128]{3,2,1,0:T(8,128)} %bitcast.44, f32[4,128,512]{2,1,0:T(8,128)} %constant.61.clone.table_ref, f32[8,224,512]{2,1,0:T(8,128)} %constant.60.clone.capacity_ref), custom_call_target="tpu_custom_call" | custom-call | tf_op jit(solution)/shard_map/strip_faces/pallas_call | solution.py:529
  384.2 6.7 %all-to-all-done.3.face_ref = f32[8,2,32,128]{3,2,1,0:T(8,128)S(1)} async-done(((f32[8,2,32,128]{3,2,1,0:T(8,128)}), f32[8,2,32,128]{3,2,1,0:T(8,128)S(1)}, u32[]{:S(2)}, u32[]{:S(2)}) %all-to-all-start.3) | async-done | bytes 262176 | tf_op jit(solution)/shard_map/all_to_all | solution.py:546
  394.8 16.3 %all-gather.5 = f32[8,64,256]{2,1,0:T(8,128)} all-gather(f32[2,64,256]{2,1,0:T(8,128)} %get-tuple-element.44), channel_id=7, replica_groups=mesh['wide'=4,'narrow'=8] {'wide'}, dimensions={0}, use_global_device_ids=true | all-gather | bytes 655360 | tf_op jit(solution)/shard_map/all_gather | solution.py:556
  411.1 48.3 %inverse_modes.3 = (f32[128,64,256]{2,1,0:T(8,128)}, f32[3,8,256]{2,1,0:T(8,128)}) custom-call(s32[1]{0:T(128)} %bitcast.index, f32[128,64,256]{2,1,0:T(8,128)} %get-tuple-element.41.modes_ref, f32[4,2,64,256]{3,2,1,0:T(8,128)} %bitcast.40, f32[8,64,256]{2,1,0:T(8,128)} %constant.57.clone.powers_ref, f32[64,256]{1,0:T(8,128)} %constant.55.clone.decay_ref, ...), custom_call_target="tpu_custom_call" | custom-call | tf_op jit(solution)/shard_map/inverse_modes/pallas_call | solution.py:567
  460.3 11.8 %psum.14 = f32[8]{0:T(128)S(1)} all-reduce(f32[8]{0:T(128)S(1)} %pad_maximum_fusion.7), channel_id=1, replica_groups=mesh['wide'=4,'narrow'=8] {'narrow'}, use_global_device_ids=true, to_apply=%region_3.0 | all-reduce | flops 8 | bytes 64 | tf_op jit(solution)/shard_map/psum | solution.py:665
  472.1 11.3 %psum.15 = f32[8]{0:T(128)S(1)} all-reduce(f32[8]{0:T(128)S(1)} %psum.14), channel_id=1, replica_groups=mesh['wide'=4,'narrow'=8] {'wide'}, use_global_device_ids=true, to_apply=%region_4.0 | all-reduce | flops 8 | bytes 64 | tf_op jit(solution)/shard_map/psum | solution.py:665
  489.9 12.0 %multiply_subtract_fusion.1 = f32[128,64,256]{2,1,0:T(8,128)} fusion(f32[128,64,256]{2,1,0:T(8,128)} %get-tuple-element.32.residual_ref.rest_0_, f32[128,64,256]{2,1,0:T(8,128)} %get-tuple-element.46.rest_1_, f32[]{:T(128)S(6)} %div.34), kind=kLoop, calls=%fused_computation.1 | loop fusion | flops 4194304 | bytes 25165828 | tf_op jit(solution)/shard_map/sub | solution.py:682
  502.5 14.4 %multiply_subtract_fusion = (f32[128,64,256]{2,1,0:T(8,128)}, f32[128,64,256]{2,1,0:T(8,128)}) fusion(f32[128,64,256]{2,1,0:T(8,128)} %get-tuple-element.48, f32[128,64,256]{2,1,0:T(8,128)} %get-tuple-element.31.field_ref.field_next, f32[]{:T(128)} %bitcast.29, f32[]{:T(128)S(6)} %add_shard_map.3, f32[]{:T(128)} %bitcast.24, f32[]{:T(128)S(6)} %div.34, ...), kind=kLoop, calls=%fused_computation | loop fusion | flops 14680064 | bytes 41943056 | tf_op jit(solution)/shard_map/sub | solution.py:683
  (70 shorter events, 41.5 us)
Async XLA Ops:
  2.4 17.6 %collective-permute-start = (f32[2,64,256]{2,1,0:T(8,128)S(1)}, f32[2,64,256]{2,1,0:T(8,128)S(1)}, u32[]{:S(2)}, u32[]{:S(2)}) collective-permute-start(f32[2,64,256]{2,1,0:T(8,128)S(1)} %pad_maximum_fusion.2), channel_id=1, source_target_pairs={{0,8},{8,16},{16,24},{1,9},{9,17},{17,25},{2,10},{10,18},{18,26},{... | collective-permute-start | bytes 393224 | tf_op jit(solution)/shard_map/ppermute | solution.py:488
  7.4 12.6 %collective-permute-start.1 = (f32[2,64,256]{2,1,0:T(8,128)S(1)}, f32[2,64,256]{2,1,0:T(8,128)S(1)}, u32[]{:S(2)}, u32[]{:S(2)}) collective-permute-start(f32[2,64,256]{2,1,0:T(8,128)S(1)} %pad_maximum_fusion.3), channel_id=1, source_target_pairs={{8,0},{16,8},{24,16},{9,1},{17,9},{25,17},{10,2},{18,10},{26,18},{... | collective-permute-start | bytes 393224 | tf_op jit(solution)/shard_map/ppermute | solution.py:488
  12.2 7.8 %collective-permute-start.2 = (f32[2,128,256]{2,1,0:T(8,128)S(1)}, f32[2,128,256]{2,1,0:T(8,128)S(1)}, u32[]{:S(2)}, u32[]{:S(2)}) collective-permute-start(f32[2,128,256]{2,1,0:T(8,128)S(1)} %pad_maximum_fusion), channel_id=1, source_target_pairs={{0,1},{1,2},{2,3},{3,4},{4,5},{5,6},{6,7},{8,9},{9,10},{10,11},{11... | collective-permute-start | bytes 786440 | tf_op jit(solution)/shard_map/ppermute | solution.py:488
  13.8 6.3 %collective-permute-start.3 = (f32[2,128,256]{2,1,0:T(8,128)S(1)}, f32[2,128,256]{2,1,0:T(8,128)S(1)}, u32[]{:S(2)}, u32[]{:S(2)}) collective-permute-start(f32[2,128,256]{2,1,0:T(8,128)S(1)} %pad_maximum_fusion.1), channel_id=1, source_target_pairs={{1,0},{2,1},{3,2},{4,3},{5,4},{6,5},{7,6},{9,8},{10,9},{11,10},{12... | collective-permute-start | bytes 786440 | tf_op jit(solution)/shard_map/ppermute | solution.py:488
  20.0 0.7 copy-start.5
  20.0 0.7 copy-start.6
  20.0 0.8 copy-start.3
  20.8 0.7 copy-start.4
  74.1 87.1 %copy-start.1 = (f32[2,64,256]{2,1,0:T(8,128)}, f32[2,64,256]{2,1,0:T(8,128)S(1)}, u32[]{:S(2)}) copy-start(f32[2,64,256]{2,1,0:T(8,128)S(1)} %pad_maximum_fusion.4.ends_ref) | copy-start | bytes 393220
  127.0 12.8 %all-to-all-start = ((f32[8,2,32,128]{3,2,1,0:T(8,128)}), f32[8,2,32,128]{3,2,1,0:T(8,128)S(1)}, u32[]{:S(2)}, u32[]{:S(2)}) async-start(f32[8,2,32,128]{3,2,1,0:T(8,128)} %strip_borders.2), calls=%async_computation | async-start | bytes 524288 | tf_op jit(solution)/shard_map/all_to_all | solution.py:524
  235.4 11.2 %collective-permute-start.6 = (f32[128,256]{1,0:T(8,128)}, f32[128,256]{1,0:T(8,128)S(1)}, u32[]{:S(2)}, u32[]{:S(2)}) collective-permute-start(f32[128,256]{1,0:T(8,128)} %get-tuple-element.38), channel_id=1, source_target_pairs={{0,1},{1,2},{2,3},{3,4},{4,5},{5,6},{6,7},{8,9},{9,10},{10,11},{11... | collective-permute-start | bytes 393224 | tf_op jit(solution)/shard_map/ppermute | solution.py:488
  236.7 9.9 %collective-permute-start.7 = (f32[128,256]{1,0:T(8,128)}, f32[128,256]{1,0:T(8,128)S(1)}, u32[]{:S(2)}, u32[]{:S(2)}) collective-permute-start(f32[128,256]{1,0:T(8,128)} %get-tuple-element.39), channel_id=1, source_target_pairs={{1,0},{2,1},{3,2},{4,3},{5,4},{6,5},{7,6},{9,8},{10,9},{11,10},{12... | collective-permute-start | bytes 393224 | tf_op jit(solution)/shard_map/ppermute | solution.py:488
  238.9 6.2 %collective-permute-start.5 = (f32[64,256]{1,0:T(8,128)S(1)}, f32[64,256]{1,0:T(8,128)S(1)}, u32[]{:S(2)}, u32[]{:S(2)}) collective-permute-start(f32[64,256]{1,0:T(8,128)S(1)} %get-tuple-element.51), channel_id=1, source_target_pairs={{8,0},{16,8},{24,16},{9,1},{17,9},{25,17},{10,2},{18,10},{26,18},{... | collective-permute-start | bytes 196616 | tf_op jit(solution)/shard_map/ppermute | solution.py:488
  240.2 6.4 %collective-permute-start.4 = (f32[64,256]{1,0:T(8,128)S(1)}, f32[64,256]{1,0:T(8,128)S(1)}, u32[]{:S(2)}, u32[]{:S(2)}) collective-permute-start(f32[64,256]{1,0:T(8,128)S(1)} %get-tuple-element.52), channel_id=1, source_target_pairs={{0,8},{8,16},{16,24},{1,9},{9,17},{17,25},{2,10},{10,18},{18,26},{... | collective-permute-start | bytes 196616 | tf_op jit(solution)/shard_map/ppermute | solution.py:488
  245.0 1.6 copy-start.9
  246.6 0.6 copy-start.10
  246.6 0.7 copy-start.7
  246.6 0.7 copy-start.8
  295.1 85.6 %copy-start = (f32[2,64,256]{2,1,0:T(8,128)}, f32[2,64,256]{2,1,0:T(8,128)S(1)}, u32[]{:S(2)}) copy-start(f32[2,64,256]{2,1,0:T(8,128)S(1)} %pad_maximum_fusion.5.ends_ref) | copy-start | bytes 393220
  312.2 71.9 %copy-start.11 = (f32[5,8,256]{2,1,0:T(8,128)S(1)}, f32[5,8,256]{2,1,0:T(8,128)}, u32[]{:S(2)}) copy-start(f32[5,8,256]{2,1,0:T(8,128)} %get-tuple-element.40) | copy-start | bytes 122884
  380.7 10.3 %all-to-all-start.3 = ((f32[8,2,32,128]{3,2,1,0:T(8,128)}), f32[8,2,32,128]{3,2,1,0:T(8,128)S(1)}, u32[]{:S(2)}, u32[]{:S(2)}) async-start(f32[8,2,32,128]{3,2,1,0:T(8,128)} %strip_faces.3), calls=%async_computation.3 | async-start | bytes 524288 | tf_op jit(solution)/shard_map/all_to_all | solution.py:546
  391.0 0.7 copy-start.2

commit v2 on v1

v2 whole, which is shorter than its diff:
```python
import functools

import jax
import jax.numpy as jnp
import ml_dtypes
import numpy as np
from jax import lax
from jax.experimental import pallas as pl
from jax.experimental.pallas import tpu as pltpu
from jax.sharding import PartitionSpec as P

PHASES = 4
F32 = jnp.float32
BF16 = jnp.bfloat16
VMEM_LIMIT = 56 * 1024 * 1024
PLANES = 16
FORWARD_TERMS = ((0, 0), (0, 1), (1, 0), (1, 1), (0, 2), (2, 0))
INVERSE_TERMS = ((0, 0), (0, 1), (1, 0))


def cosine_table(length):
    m = np.arange(length)[:, None]
    n = np.arange(length)[None, :]
    weight = np.where(m == 0, np.sqrt(1.0 / length), np.sqrt(2.0 / length))
    return weight * np.cos(np.pi * (m * (2 * n + 1) % (4 * length)) / (2.0 * length))


def eigen_values(length):
    return 4.0 * np.sin(np.pi * np.arange(length) / (2.0 * length)) ** 2


def pieces(matrix, count=3):
    rest = np.asarray(matrix, np.float64)
    result = []
    for _ in range(count):
        piece = rest.astype(np.float32).astype(ml_dtypes.bfloat16)
        result.append(piece)
        rest = rest - piece.astype(np.float64)
    return np.stack(result)


def make_tables(size_x, size_y, size_z, wide, narrow):
    length_x = size_x * wide
    group = min(max(256 // size_y, 1), size_x)
    parity = np.concatenate([np.arange(0, size_y, 2), np.arange(1, size_y, 2)])
    strip = cosine_table(size_y)[parity]
    block_y = np.kron(np.eye(group), strip)
    table_z = cosine_table(size_z)
    shift = 4.0 * np.sin(np.pi / (2.0 * length_x)) ** 2
    eig_z = eigen_values(size_z)
    sigma = shift + eigen_values(size_y)[parity][:, None] + eig_z[None, :]
    theta = 2.0 * np.arcsinh(np.sqrt(sigma) / 2.0)
    decay = np.exp(-theta)
    kappa = 1.0 / (2.0 * np.sinh(theta))
    step = np.exp(-theta * size_x)
    total = -np.expm1(-2.0 * wide * size_x * theta)
    powers = np.stack([step**t / total for t in range(2 * wide)])
    border = np.broadcast_to(strip[:, :1], sigma.shape)
    eta = 2.0 * np.arcsinh(
        np.sqrt(shift + eig_z[:, None] + eigen_values(length_x)[None, :]) / 2.0
    )
    fade = np.exp(-eta * size_y)
    half_angle = np.pi * np.arange(1, narrow) / (2.0 * narrow)
    capacity = (np.tanh(eta / 2.0) * -np.expm1(-2.0 * eta * size_y))[None] / (
        (np.expm1(-eta * size_y) ** 2)[None]
        + 4.0 * fade[None] * (np.sin(half_angle) ** 2)[:, None, None]
    )
    devices = wide * narrow
    part = size_z // devices
    capacity = capacity.reshape(narrow - 1, devices, part, length_x).transpose(1, 0, 2, 3)
    k = np.arange(1, narrow)
    sines = np.sqrt(2.0 / narrow) * np.sin(np.pi * k[:, None] * k[None, :] / narrow)
    table_x = cosine_table(length_x).T.reshape(wide, size_x, length_x)
    by_mode = lambda left, right: np.concatenate([left.T, right.T], axis=1).reshape(devices, part, 2 * size_y)
    mix = np.stack(
        [
            np.stack(
                [
                    np.stack(
                        [
                            by_mode(powers[(d - 1 - b) % (2 * wide)], powers[(b - 1 - d) % (2 * wide)]),
                            by_mode(powers[(d + b) % (2 * wide)], powers[(2 * wide - 2 - b - d) % (2 * wide)]),
                        ],
                        axis=1,
                    )
                    for b in range(wide)
                ],
                axis=1,
            )
            for d in range(wide)
        ],
        axis=1,
    )
    even = np.broadcast_to((np.arange(size_y) < (size_y + 1) // 2)[:, None], sigma.shape)
    row, end = (border * decay, border * kappa)
    twice = lambda values: by_mode(values, values)
    f32 = lambda a: np.asarray(a, np.float32)
    return dict(
        group=group,
        planes=min(PLANES, size_x),
        z_fwd=pieces(table_z.T),
        z_inv=pieces(table_z, 2),
        y_fwd=pieces(block_y),
        y_inv=pieces(block_y.T, 2),
        theta=f32(theta.T.reshape(devices, part, size_y)),
        decay=f32(decay),
        kappa=f32(kappa),
        border=f32(border),
        border_kappa=f32(end),
        mix=f32(mix),
        row_even=f32(twice(np.where(even, row, 0.0))),
        row_odd=f32(twice(np.where(even, 0.0, row))),
        row_dot=f32(twice(decay / kappa)),
        inverse_kappa=f32(1.0 / kappa),
        mean_scale=float(np.sqrt(size_y * size_z) / (shift * kappa[0, 0])),
        end_even=f32(twice(np.where(even, end, 0.0))),
        end_odd=f32(twice(np.where(even, 0.0, end))),
        capacity=f32(capacity.reshape(devices, (narrow - 1) * part, length_x)),
        sines=sines,
        table_x=f32(table_x),
    )


def split(values, count):
    result = [values.astype(BF16)]
    rest = values
    for _ in range(count - 1):
        rest = rest - result[-1].astype(F32)
        result.append(rest.astype(BF16))
    return result


def product_right(values, matrix_ref, terms):
    parts = split(values, 1 + max(a for a, _ in terms))
    total = None
    for a, b in reversed(terms):
        term = jnp.dot(parts[a], matrix_ref[b], preferred_element_type=F32)
        total = term if total is None else total + term
    return total


def product_left(matrix_ref, values, terms):
    parts = split(values, 1 + max(a for a, _ in terms))
    total = None
    for a, b in reversed(terms):
        term = jnp.dot(matrix_ref[b], parts[a], preferred_element_type=F32)
        total = term if total is None else total + term
    return total


def lookup(phase, scal, component):
    base = 4 * component
    picked = jnp.where(phase == 2.0, scal[base + 2], scal[base + 3])
    picked = jnp.where(phase == 1.0, scal[base + 1], picked)
    return jnp.where(phase == 0.0, scal[base], picked)


def forward_modes(first, block, z_ref, y_ref, kappa_ref, decay_ref, modes_ref, ahead_ref, back_ref, power):
    rows = block[0].shape[0]
    flat = jnp.concatenate(block, axis=0)
    flat = product_right(flat, z_ref, FORWARD_TERMS)
    flat = product_left(y_ref, flat, FORWARD_TERMS)
    kappa, decay = (kappa_ref[...], decay_ref[...])
    ahead, back, weight = (ahead_ref[...], back_ref[...], power[...])
    for j in range(len(block)):
        scaled = flat[j * rows : (j + 1) * rows] * kappa
        modes_ref[first + j] = scaled
        ahead = decay * ahead + scaled
        back = back + weight * scaled
        weight = weight * decay
    ahead_ref[...] = ahead
    back_ref[...] = back
    power[...] = weight


def fold(values):
    rows, depth = values.shape
    return jnp.sum(values.reshape(rows // 8, 8, depth), axis=0)


def residual_kernel(
    group, planes,
    scal, phase_ref, phase_next, field_ref, field_next, x_before, x_after, y_before, y_after,
    z_mat, y_mat, kappa_ref, decay_ref,
    residual_ref, modes_ref, fx_ref, fy_ref, fz_ref, fx_low, fy_low, ahead_ref, back_ref,
    flux_low, power,
):
    step = pl.program_id(0)
    rows, depth = flux_low.shape
    gx, gy, gz = scal[12], scal[13], scal[14]
    flag_xb, flag_xa, flag_yb, flag_ya = scal[15], scal[16], scal[17], scal[18]
    row = lax.broadcasted_iota(jnp.int32, (rows, depth), 0)
    lane = lax.broadcasted_iota(jnp.int32, (rows, depth), 1)

    @pl.when(step == 0)
    def _():
        face = flag_xb / (lookup(x_before[0], scal, 0) + lookup(phase_ref[0].astype(F32), scal, 0))
        fx_low[...] = face
        flux_low[...] = face * (field_ref[0] - x_before[1] + gx)
        ahead_ref[...] = jnp.zeros_like(ahead_ref)
        back_ref[...] = jnp.zeros_like(back_ref)
        power[...] = jnp.ones_like(power)

    last = step == pl.num_programs(0) - 1
    end_phase = jnp.where(last, x_after[0], phase_next[0].astype(F32))
    end_field = jnp.where(last, x_after[1], field_next[0])
    flag_end = jnp.where(last, flag_xa, 1.0)
    flux_x_low = flux_low[...]
    hx = lookup(phase_ref[0].astype(F32), scal, 0)
    done = []
    for j in range(planes):
        x = step * planes + j
        phase = phase_ref[j].astype(F32)
        field = field_ref[j]
        if j + 1 < planes:
            hx_next = lookup(phase_ref[j + 1].astype(F32), scal, 0)
            field_up = field_ref[j + 1]
            fx = 1.0 / (hx + hx_next)
        else:
            hx_next = lookup(end_phase, scal, 0)
            field_up = end_field
            fx = flag_end / (hx + hx_next)
        flux_x = fx * (field_up - field + gx)
        total = flux_x - flux_x_low
        flux_x_low, hx = flux_x, hx_next
        fx_ref[j] = fx

        hy = lookup(phase, scal, 1)
        hy_up = jnp.where(
            row == rows - 1,
            lookup(y_after[0, pl.ds(x, 1), :], scal, 1),
            pltpu.roll(hy, rows - 1, 0),
        )
        fy = jnp.where(row == rows - 1, flag_ya, 1.0) / (hy + hy_up)
        v_up = jnp.where(row == rows - 1, y_after[1, pl.ds(x, 1), :], pltpu.roll(field, rows - 1, 0))
        flux_y = fy * (v_up - field + gy)
        face = flag_yb / (lookup(y_before[0, pl.ds(x, 1), :], scal, 1) + hy[0:1])
        low = face * (field[0:1] - y_before[1, pl.ds(x, 1), :] + gy)
        total = total + (flux_y - jnp.where(row == 0, low, pltpu.roll(flux_y, 1, 0)))
        fy_ref[j] = fy
        fy_low[pl.ds(x, 1), :] = face

        hz = lookup(phase, scal, 2)
        fz = jnp.where(lane == depth - 1, 0.0, 1.0 / (hz + pltpu.roll(hz, depth - 1, 1)))
        flux_z = fz * (pltpu.roll(field, depth - 1, 1) - field + gz)
        total = total + (flux_z - pltpu.roll(flux_z, 1, 1))
        fz_ref[j] = fz
        residual_ref[j] = total
        done.append(total)
        if len(done) == group:
            forward_modes(
                j + 1 - group, done, z_mat, y_mat, kappa_ref, decay_ref, modes_ref, ahead_ref, back_ref, power
            )
            done = []
    flux_low[...] = flux_x_low


def image_kernel(
    group, planes,
    field_ref, field_next, residual_ref, fx_ref, fy_ref, fz_ref, fx_low, fy_low,
    x_before, x_after, y_jump, z_mat, y_mat, kappa_ref, decay_ref,
    image_ref, modes_ref, ahead_ref, back_ref, sums_ref,
    flux_low, power,
):
    step = pl.program_id(0)
    rows, depth = flux_low.shape
    row = lax.broadcasted_iota(jnp.int32, (rows, depth), 0)

    @pl.when(step == 0)
    def _():
        flux_low[...] = fx_low[...] * (field_ref[0] - x_before[...])
        ahead_ref[...] = jnp.zeros_like(ahead_ref)
        back_ref[...] = jnp.zeros_like(back_ref)
        power[...] = jnp.ones_like(power)
        sums_ref[...] = jnp.zeros_like(sums_ref)

    last = step == pl.num_programs(0) - 1
    end_field = jnp.where(last, x_after[...], field_next[0])
    flux_x_low = flux_low[...]
    sums = [sums_ref[i] for i in range(5)]
    done = []
    for j in range(planes):
        x = step * planes + j
        field = field_ref[j]
        field_up = field_ref[j + 1] if j + 1 < planes else end_field
        flux_x = fx_ref[j] * (field_up - field)
        total = flux_x_low - flux_x
        flux_x_low = flux_x
        jump = jnp.where(row == rows - 1, y_jump[1, pl.ds(x, 1), :], pltpu.roll(field, rows - 1, 0) - field)
        flux_y = fy_ref[j] * jump
        low = fy_low[pl.ds(x, 1), :] * y_jump[0, pl.ds(x, 1), :]
        total = total + (jnp.where(row == 0, low, pltpu.roll(flux_y, 1, 0)) - flux_y)
        flux_z = fz_ref[j] * (pltpu.roll(field, depth - 1, 1) - field)
        total = total + (pltpu.roll(flux_z, 1, 1) - flux_z)
        image_ref[j] = total
        res = residual_ref[j]
        for i, term in enumerate((res * field, res, field * total, total, field)):
            sums[i] = sums[i] + fold(term)
        done.append(total)
        if len(done) == group:
            forward_modes(
                j + 1 - group, done, z_mat, y_mat, kappa_ref, decay_ref, modes_ref, ahead_ref, back_ref, power
            )
            done = []
    for i in range(5):
        sums_ref[i] = sums[i]
    flux_low[...] = flux_x_low


def local_kernel(devices, planes, summed, modes_ref, ahead_ref, back_ref, decay_ref, border_ref, *rest):
    if summed:
        sums_ref, weight_ref, out_ref, run, kept, rows_ref, dots, corner = rest
    else:
        out_ref, run, kept, rows_ref = rest
    phase, step = pl.program_id(0), pl.program_id(1)
    blocks = pl.num_programs(1)
    decay = decay_ref[...]
    half = decay.shape[0] // 2

    @pl.when(step == 0)
    def _():
        run[...] = jnp.zeros_like(run)
        if summed:
            dots[...] = jnp.zeros_like(dots)

    @pl.when(phase == 0)
    def _():
        value = run[...]
        for j in range(planes):
            value = modes_ref[j] + decay * value
            kept[step * planes + j] = value
        run[...] = value
        if summed:
            lowest = modes_ref[0, :8, :128]
            for j in range(1, planes):
                lowest = lowest + modes_ref[j, :8, :128]
            corner[...] = jnp.where(step == 0, lowest, corner[...] + lowest)

    @pl.when(phase == 1)
    def _():
        value = run[...]
        border = border_ref[...]
        first = (blocks - 1 - step) * planes
        total = dots[...] if summed else None
        for j in reversed(range(planes)):
            passed = decay * value
            mode = kept[first + j] + passed
            if summed:
                total = total + modes_ref[j] * mode
            mode = mode * border
            value = modes_ref[j] + passed
            rows_ref[0, pl.ds(first + j, 1), :] = jnp.sum(mode[:half], axis=0, keepdims=True)
            rows_ref[1, pl.ds(first + j, 1), :] = jnp.sum(mode[half:], axis=0, keepdims=True)
        run[...] = value
        if summed:
            dots[...] = total

    @pl.when((phase == 1) & (step == blocks - 1))
    def _():
        part, width = out_ref.shape[2:]
        ends = jnp.concatenate([ahead_ref[...], back_ref[...]], axis=0)
        for slot, turned in enumerate((rows_ref[0].T, rows_ref[1].T, ends.T)):
            for j in range(devices):
                out_ref[j, slot] = turned[j * part : (j + 1) * part]
        if summed:
            lane = lax.broadcasted_iota(jnp.int32, (part, width), 1)
            packed = jnp.zeros((part, width), F32)
            for i in range(5):
                packed = jnp.where(lane == i, jnp.sum(sums_ref[i]), packed)
            packed = jnp.where(lane == 5, jnp.sum(dots[...] * weight_ref[...]), packed)
            packed = jnp.where(lane == 6, jnp.sum(corner[:1, :1]), packed)
            for j in range(devices):
                out_ref[j, 3] = packed


def faces_kernel(
    wide, narrow, part, sines, summed,
    device, got_ref, table_ref, capacity_ref, power_ref, mix_ref, row_even, row_odd, end_even, end_odd, row_dot,
    out_ref, jumps, modes,
):
    devices = wide * narrow
    width = got_ref.shape[1]
    slots = 4 if summed else 3
    faces = narrow - 1
    highest = dict(preferred_element_type=F32, precision=lax.Precision.HIGHEST)

    def take(ref, slot, mode, count):
        return ref[pl.ds(slot * part + mode, devices, stride=count * part), :]

    def incoming(ends, mode):
        swapped = pltpu.roll(ends, width // 2, 1)
        result = []
        for mine in range(wide):
            total = None
            for block in range(wide):
                at = slice(block * narrow, (block + 1) * narrow)
                term = mix_ref[0, mine, block, 0, pl.ds(mode, 1), :] * ends[at]
                term = term + mix_ref[0, mine, block, 1, pl.ds(mode, 1), :] * swapped[at]
                total = term if total is None else total + term
            result.append(total)
        return jnp.concatenate(result, axis=0)

    inner = None
    for mode in range(part):
        ends = take(got_ref, 2, mode, slots)
        entering = incoming(ends, mode)
        if summed:
            term = entering * pltpu.roll(ends, width // 2, 1) * row_dot[0, pl.ds(mode, 1), :]
            inner = term if inner is None else inner + term
        both = jnp.concatenate(
            [entering * row_even[0, pl.ds(mode, 1), :], entering * row_odd[0, pl.ds(mode, 1), :]], axis=0
        )
        added = jnp.dot(both, power_ref[mode], **highest)
        even = take(got_ref, 0, mode, slots) + added[:devices]
        odd = take(got_ref, 1, mode, slots) + added[devices:]
        jump = pltpu.roll(even + odd, devices - 1, 0) - (even - odd)
        jumps[pl.ds(mode, devices, stride=part), :] = jump
    mixed = None
    for block in range(wide):
        strips = [jumps[pl.ds((block * narrow + i) * part, part), :] for i in range(faces)]
        for k in range(faces):
            acc = None
            for i in range(faces):
                term = strips[i] * float(sines[k, i])
                acc = term if acc is None else acc + term
            modes[pl.ds(k * part, part), :] = acc
        term = jnp.dot(modes[...], table_ref[block], **highest)
        mixed = term if mixed is None else mixed + term
    plain = mixed
    mixed = mixed * capacity_ref[0]
    for block in range(wide):
        modes[...] = lax.dot_general(mixed, table_ref[block], (((1,), (1,)), ((), ())), **highest)
        solved = []
        for k in range(faces):
            acc = None
            for i in range(faces):
                term = modes[pl.ds(i * part, part), :] * float(sines[k, i])
                acc = term if acc is None else acc + term
            solved.append(acc)
        for strip in range(narrow):
            below = solved[strip - 1] if strip > 0 else jnp.zeros_like(solved[0])
            above = solved[strip] if strip < faces else jnp.zeros_like(solved[0])
            at = (block * narrow + strip) * slots * part
            out_ref[pl.ds(at, part), :] = above - below
            out_ref[pl.ds(at + part, part), :] = -(above + below)
    for mode in range(part):
        both = jnp.concatenate([take(out_ref, 0, mode, slots), take(out_ref, 1, mode, slots)], axis=0)
        added = lax.dot_general(both, power_ref[mode], (((1,), (1,)), ((), ())), **highest)
        added = pltpu.roll(added, width // 2, 1)
        ends = take(got_ref, 2, mode, slots) + end_even[0, pl.ds(mode, 1), :] * added[:devices]
        ends = ends + end_odd[0, pl.ds(mode, 1), :] * added[devices:]
        out_ref[pl.ds(2 * part + mode, devices, stride=slots * part), :] = incoming(ends, mode)
    if summed:
        totals = jnp.sum(take(got_ref, 3, 0, slots), axis=0, keepdims=True)
        share = jnp.sum(inner) - jnp.sum(plain * mixed)
        lane = lax.broadcasted_iota(jnp.int32, (part, width), 1)
        packed = jnp.where(lane == 7, share, jnp.broadcast_to(totals, (part, width)))
        for j in range(devices):
            out_ref[pl.ds((j * slots + 3) * part, part), :] = packed


def inverse_kernel(
    group, planes, dotted, voxels, mean_scale,
    faces_ref, modes_ref, decay_ref, scale_ref, y_mat, z_mat, *rest,
):
    if dotted:
        scal, residual_ref, image_ref, along_ref, start_ref = rest[:5]
        out_ref, solution_ref, next_ref = rest[5:8]
    else:
        out_ref, before_ref, after_ref, jump_ref = rest[:4]
    run, kept, fixed, rows_ref, entering, turned, factors = rest[-7:]
    phase, step = pl.program_id(0), pl.program_id(1)
    blocks = pl.num_programs(1)
    decay = decay_ref[...]
    rows, depth = decay.shape
    half = rows // 2

    @pl.when((phase == 0) & (step == 0))
    def _():
        devices, _, part, _ = faces_ref.shape
        for slot in range(3):
            for j in range(devices):
                turned[pl.ds(j * part, part), :] = faces_ref[j, slot]
            if slot < 2:
                rows_ref[slot] = turned[...].T
            else:
                entering[...] = turned[...].T
        run[...] = entering[pl.ds(0, rows), :]
        if dotted:
            shared = faces_ref[0, 3]
            for j in range(1, devices):
                shared = shared + faces_ref[j, 3]
            lane = lax.broadcasted_iota(jnp.int32, shared.shape, 1)[:1]

            def value(i):
                source = shared if i == 7 else faces_ref[0, 3]
                return jnp.sum(jnp.where(lane == i, source[:1], 0.0), axis=1, keepdims=True)

            base = scal[0]
            mean = value(4) / voxels
            mean_turned = value(6) * (mean_scale / voxels)
            rz_now = value(0) - mean * value(1)
            alpha = rz_now / (value(2) - mean * value(3))
            square = base * (value(5) + value(7)) - mean_turned * value(3)
            ratio = alpha * (alpha * square) / rz_now
            for i, factor in enumerate((alpha, mean, ratio, ratio * mean - alpha * mean_turned)):
                factors[pl.ds(i, 1), :] = jnp.broadcast_to(factor, (1, depth))

    @pl.when(phase == 0)
    def _():
        value = run[...]
        scale = scale_ref[...]
        for j in range(planes):
            x = step * planes + j
            face = jnp.concatenate(
                [
                    jnp.broadcast_to(rows_ref[0, pl.ds(x, 1), :], (half, depth)),
                    jnp.broadcast_to(rows_ref[1, pl.ds(x, 1), :], (half, depth)),
                ],
                axis=0,
            )
            mode = modes_ref[j] + scale * face
            value = mode + decay * value
            fixed[x] = mode
            kept[x] = value
        run[...] = value

    @pl.when((phase == 1) & (step == 0))
    def _():
        run[...] = entering[pl.ds(rows, rows), :]

    @pl.when(phase == 1)
    def _():
        value = run[...]
        first = (blocks - 1 - step) * planes
        if dotted:
            alpha, mean, ratio, offset = [
                jnp.broadcast_to(factors[pl.ds(i, 1), :], (rows, depth)) for i in range(4)
            ]
        for start in reversed(range(0, planes, group)):
            modes = [None] * group
            for j in reversed(range(group)):
                x = first + start + j
                passed = decay * value
                value = fixed[x] + passed
                modes[j] = kept[x] + passed
            flat = jnp.concatenate(modes, axis=0)
            flat = product_left(y_mat, flat, INVERSE_TERMS)
            flat = product_right(flat, z_mat, INVERSE_TERMS)
            for j in range(group):
                at = start + j
                plane = flat[j * rows : (j + 1) * rows]
                if dotted:
                    along = along_ref[at]
                    next_ref[at] = residual_ref[at] - alpha * image_ref[at]
                    solution_ref[at] = start_ref[at] + alpha * (along - mean)
                    plane = (ratio * along - offset) - alpha * plane
                out_ref[at] = plane
        run[...] = value

    if not dotted:
        @pl.when((phase == 1) & (step == blocks - 1))
        def _():
            before = entering[pl.ds(0, rows), :] + decay * run[...]
            after = entering[pl.ds(rows, rows), :] + decay * kept[blocks * planes - 1]
            flat = jnp.concatenate([before, after] * (group // 2), axis=0)
            flat = product_left(y_mat, flat, INVERSE_TERMS)
            flat = product_right(flat, z_mat, INVERSE_TERMS)
            before_ref[...] = flat[:rows]
            after_ref[...] = flat[rows : 2 * rows]
            jump_ref[0] = product_right(-0.5 * (rows_ref[0] + rows_ref[1]), z_mat, INVERSE_TERMS)
            jump_ref[1] = product_right(0.5 * (rows_ref[0] - rows_ref[1]), z_mat, INVERSE_TERMS)


def whole(shape, single=False):
    mode = dict(pipeline_mode=pl.Buffered(1)) if single else {}
    return pl.BlockSpec(shape, lambda *_: (0,) * len(shape), **mode)


def shape_of(*dims):
    return jax.ShapeDtypeStruct(dims, F32)


def params(dims):
    return pltpu.CompilerParams(dimension_semantics=("arbitrary",) * dims, vmem_limit_bytes=VMEM_LIMIT)


def neighbours(axis):
    devices = lax.axis_size(axis)
    up = [(i, i + 1) for i in range(devices - 1)]
    return up, [(j, i) for i, j in up]


def exchange(first, last, axis):
    up, down = neighbours(axis)
    return lax.ppermute(last, axis, up), lax.ppermute(first, axis, down)


def solve(modes, ahead, back, tab, device, sums=None, final=None):
    size_x, size_y, size_z = modes.shape
    wide, narrow = lax.axis_size("wide"), lax.axis_size("narrow")
    devices = wide * narrow
    group, planes = tab["group"], tab["planes"]
    blocks = size_x // planes
    part = size_z // devices
    plane = (size_y, size_z)
    block = (planes,) + plane
    summed = sums is not None
    slots = 4 if summed else 3
    field = shape_of(size_x, *plane)
    sweep = lambda p, i, *_: (jnp.where(p == 0, i, blocks - 1 - i), 0, 0)
    packed = (devices, slots, part, size_x)
    sent = pl.pallas_call(
        functools.partial(local_kernel, devices, planes, summed),
        grid=(2, blocks),
        out_shape=shape_of(*packed),
        in_specs=[pl.BlockSpec(block, sweep)]
        + [whole(plane)] * 4
        + [whole((5, 8, size_z)), whole(plane)] * summed,
        out_specs=whole(packed),
        scratch_shapes=[
            pltpu.VMEM(plane, F32),
            pltpu.VMEM((size_x,) + plane, F32),
            pltpu.VMEM((2, size_x, size_z), F32),
        ]
        + [pltpu.VMEM(plane, F32), pltpu.VMEM((8, 128), F32)] * summed,
        compiler_params=params(2),
        name="strip_borders",
    )(modes, ahead, back, tab["decay"], tab["border"], *([sums, tab["inverse_kappa"]] if summed else []))
    got = lax.all_to_all(sent, ("wide", "narrow"), split_axis=0, concat_axis=0, tiled=True)
    faces = narrow - 1
    length_x = wide * size_x
    flat = (devices * slots * part, size_x)
    mine = lambda shape: pl.BlockSpec((1,) + shape, lambda i, idx: (idx[0],) + (0,) * len(shape))
    solved = pl.pallas_call(
        functools.partial(faces_kernel, wide, narrow, part, tab["sines"], summed),
        out_shape=shape_of(*flat),
        grid_spec=pltpu.PrefetchScalarGridSpec(
            num_scalar_prefetch=1,
            grid=(1,),
            in_specs=[
                whole(flat),
                whole((wide, size_x, length_x)),
                mine((faces * part, length_x)),
                whole((part, 2 * size_y, size_x)),
                mine((wide, wide, 2, part, size_x)),
            ]
            + [mine((part, size_x))] * 5,
            out_specs=whole(flat),
            scratch_shapes=[
                pltpu.VMEM((devices * part, size_x), F32),
                pltpu.VMEM((faces * part, size_x), F32),
            ],
        ),
        compiler_params=params(1),
        name="strip_faces",
    )(
        device, got.reshape(flat), tab["table_x"], tab["capacity"], tab["decay_powers"], tab["mix"],
        tab["row_even"], tab["row_odd"], tab["end_even"], tab["end_odd"], tab["row_dot"],
    )
    mine_now = lax.all_to_all(
        solved.reshape(packed), ("wide", "narrow"), split_axis=0, concat_axis=0, tiled=True
    )
    back_map = lambda p, i, *_: (jnp.where(p == 0, blocks - 1, blocks - 1 - i), 0, 0)
    ahead_map = lambda p, i, *_: (jnp.where(p == 0, i, blocks - 1), 0, 0)
    behind = pl.BlockSpec(block, back_map)
    operands = [mine_now, modes, tab["decay"], tab["border_kappa"], tab["y_inv"], tab["z_inv"]]
    in_specs = [whole(mine_now.shape), pl.BlockSpec(block, ahead_map), whole(plane), whole(plane)]
    in_specs += [whole(tab["y_inv"].shape), whole(tab["z_inv"].shape)]
    if summed:
        operands += final
        in_specs += [pl.BlockSpec(memory_space=pltpu.SMEM)] + [behind] * 4
        out_shape = (field,) * 3
        out_specs = (behind,) * 3
    else:
        jumps = (2, size_x, size_z)
        out_shape = (field, shape_of(*plane), shape_of(*plane), shape_of(*jumps))
        out_specs = (behind, whole(plane), whole(plane), whole(jumps))
    voxels = float(devices * size_x * size_y * size_z)
    return pl.pallas_call(
        functools.partial(inverse_kernel, group, planes, summed, voxels, tab["mean_scale"]),
        grid=(2, blocks),
        out_shape=out_shape,
        in_specs=in_specs,
        out_specs=out_specs,
        scratch_shapes=[
            pltpu.VMEM(plane, F32),
            pltpu.VMEM((size_x,) + plane, F32),
            pltpu.VMEM((size_x,) + plane, F32),
            pltpu.VMEM((2, size_x, size_z), F32),
            pltpu.VMEM((2 * size_y, size_z), F32),
            pltpu.VMEM((size_z, size_x), F32),
            pltpu.VMEM((8, size_z), F32),
        ],
        compiler_params=params(2),
        name="inverse_modes",
    )(*operands)


def on_device(phase_ids, conduct_table, gradient, start_field):
    size_x, size_y, size_z = start_field.shape
    wide, narrow = lax.axis_size("wide"), lax.axis_size("narrow")
    tab = make_tables(size_x, size_y, size_z, wide, narrow)
    tab = {k: jnp.asarray(v) if isinstance(v, np.ndarray) and k != "sines" else v for k, v in tab.items()}
    group, planes = tab["group"], tab["planes"]
    blocks = size_x // planes
    plane = (size_y, size_z)
    block = (planes,) + plane
    wide_at, narrow_at = lax.axis_index("wide"), lax.axis_index("narrow")
    device = (wide_at * narrow + narrow_at).astype(jnp.int32)
    theta = lax.dynamic_index_in_dim(tab["theta"], device, 0, False)[:, :, None]
    along_x = jnp.arange(size_x, dtype=F32)
    tab["decay_powers"] = jnp.concatenate(
        [jnp.exp(-theta * along_x), jnp.exp(-theta * (size_x - 1.0 - along_x))], axis=1
    )
    device = device.reshape(1)
    flags = jnp.stack([wide_at > 0, wide_at < wide - 1, narrow_at > 0, narrow_at < narrow - 1])
    scal = jnp.concatenate([(0.5 / conduct_table).T.reshape(-1), gradient, flags.astype(F32)])
    kappa = tab["kappa"] / jnp.mean(conduct_table)

    edge = lambda dim, at: jnp.stack(
        [lax.index_in_dim(phase_ids, at, dim, False).astype(F32), lax.index_in_dim(start_field, at, dim, False)]
    )
    x_before, x_after = exchange(edge(0, 0), edge(0, size_x - 1), "wide")
    y_before, y_after = exchange(edge(1, 0), edge(1, size_y - 1), "narrow")

    main = pl.BlockSpec(block, lambda i: (i, 0, 0))
    following = pl.BlockSpec((1,) + plane, lambda i: (jnp.minimum((i + 1) * planes, size_x - 1), 0, 0))
    field_shape = shape_of(size_x, *plane)
    matrices = [whole(tab["z_fwd"].shape), whole(tab["y_fwd"].shape), whole(plane), whole(plane)]
    carried = [pltpu.VMEM(plane, F32), pltpu.VMEM(plane, F32)]
    residual, modes, fx, fy, fz, fx_low, fy_low, ahead, back = pl.pallas_call(
        functools.partial(residual_kernel, group, planes),
        grid=(blocks,),
        out_shape=(field_shape,) * 5 + (shape_of(*plane), shape_of(size_x, size_z)) + (shape_of(*plane),) * 2,
        in_specs=[pl.BlockSpec(memory_space=pltpu.SMEM), main, following, main, following]
        + [whole((2,) + plane)] * 2
        + [whole((2, size_x, size_z))] * 2
        + matrices,
        out_specs=(main,) * 5 + (whole(plane), whole((size_x, size_z))) + (whole(plane),) * 2,
        scratch_shapes=carried,
        compiler_params=params(1),
        name="residual_modes",
    )(
        scal, phase_ids, phase_ids, start_field, start_field, x_before, x_after, y_before, y_after,
        tab["z_fwd"], tab["y_fwd"], kappa, tab["decay"],
    )
    along, xb, xa, jumps = solve(modes, ahead, back, tab, device)

    image, modes, ahead, back, sums = pl.pallas_call(
        functools.partial(image_kernel, group, planes),
        grid=(blocks,),
        out_shape=(field_shape,) * 2 + (shape_of(*plane),) * 2 + (shape_of(5, 8, size_z),),
        in_specs=[main, following] + [main] * 4
        + [whole(plane), whole((size_x, size_z))]
        + [whole(plane)] * 2
        + [whole((2, size_x, size_z))]
        + matrices,
        out_specs=(main,) * 2 + (whole(plane),) * 2 + (whole((5, 8, size_z)),),
        scratch_shapes=carried,
        compiler_params=params(1),
        name="image_modes",
    )(
        along, along, residual, fx, fy, fz, fx_low, fy_low, xb, xa, jumps,
        tab["z_fwd"], tab["y_fwd"], kappa, tab["decay"],
    )
    base = jnp.mean(conduct_table).reshape(1)
    new_direction, result, residual_next = solve(
        modes, ahead, back, tab, device, sums, [base, residual, image, along, start_field]
    )
    return result, residual_next, new_direction


def solution(mesh):
    placed = (P("wide", "narrow", None), P(), P(), P("wide", "narrow", None))
    return jax.shard_map(
        on_device,
        mesh=mesh,
        in_specs=placed,
        out_specs=(P("wide", "narrow", None),) * 3,
        check_vma=False,
    )
```

time: 522 us -> 247 us (0.47)
  Pallas kernels: 276 us -> 146 us
  blocking collectives: 147 us -> 54.2 us
  other arithmetic: 34.9 us -> 6.81 us
  starting transfers between devices: 26.7 us -> 18.7 us
  between operations: 8 us -> 1.48 us
    pallas_call x10 -> x8, Pallas kernels: 276 us -> 146 us  [the longest x2 49.4 us: solve(): pl.pallas_call(functools.partial(inverse_kernel, group, planes, summed, v...]
    all_gather x6 -> x0, blocking collectives: 101 us -> none  [the longest x2 35.1 us: solve(): ends_all = lax.all_gather(ends, 'wide', axis=0)]
    all_to_all x2 -> x3, blocking collectives: 23.5 us -> 54.2 us  [the longest x2 35.3 us: solve(): lax.all_to_all(solved.reshape(packed), ('wide', 'narrow'), split_axis=0,...]
    sub x2 -> x1, other arithmetic: 26.4 us -> 0.01 us  [on_device(): size_x - 1.0 - along_x]
    psum x2 -> x0, blocking collectives: 23 us -> none  [on_device(): sums = lax.psum(lax.psum(sums, 'narrow'), 'wide')]
    ppermute x8 -> x4, starting transfers between devices: 17.4 us -> 8.99 us  [exchange(): return (lax.ppermute(last, axis, up), lax.ppermute(first, axis, down))]
    all_to_all x2 -> x1, waiting for transfers between devices: 13.1 us -> 11.5 us  [solve(): lax.all_to_all(sent, ('wide', 'narrow'), split_axis=0, concat_axis=0, til...]
  transfers between devices with their start and end apart: 10 -> 5, of which waited for: 4 -> 1; matrix products, arithmetic and copies ran while one was open for 2% -> 4% of each run, Pallas kernels for 0% -> 0%
where the time goes in v2:
time: 247 us; the launch traced here: 246 us
  Pallas kernels  146 us (59%)
  blocking collectives  54.2 us (22%)
  starting transfers between devices  18.7 us (8%)
  waiting for transfers between devices  11.5 us (5%)
  other arithmetic  6.81 us (3%)
  local copies, waits for them, and re-layouts  6.73 us (3%)
    pallas_call x2, Pallas kernels, solve(): pl.pallas_call(functools.partial(inverse_kernel, group, planes, summed, v...  49.4 us
    all_to_all x2, blocking collectives, solve(): lax.all_to_all(solved.reshape(packed), ('wide', 'narrow'), split_axis=0,...  35.3 us
    pallas_call x1, Pallas kernels, on_device(): pl.pallas_call(functools.partial(residual_kernel, group, planes), grid=(b...  30 us
    pallas_call x1, Pallas kernels, on_device(): pl.pallas_call(functools.partial(image_kernel, group, planes), grid=(bloc...  28 us
    pallas_call x2, Pallas kernels, solve(): pl.pallas_call(functools.partial(local_kernel, devices, planes, summed),...  26.7 us
    all_to_all x1, blocking collectives, solve(): lax.all_to_all(sent, ('wide', 'narrow'), split_axis=0, concat_axis=0, til...  18.8 us
    pallas_call x2, Pallas kernels, solve(): pl.pallas_call(functools.partial(faces_kernel, wide, narrow, part, tab['s...  12.2 us
    all_to_all x1, waiting for transfers between devices, solve(): lax.all_to_all(sent, ('wide', 'narrow'), split_axis=0, concat_axis=0, til...  11.5 us
  transfers between devices with their start and end apart: 5, of which 1 were waited for; matrix products, arithmetic and copies ran while one was open for 4% of the time, Pallas kernels for 0%

profile of v2, /device:TPU:0, one launch (start us, length us, event | category | flops | bytes accessed | tf_op | source)
XLA Modules:
  0.0 245.7 jit_solution(6213728593956367241)
XLA Ops:
  0.6 0.9 slice_convert_fusion
  1.5 0.9 fusion.4
  2.4 4.9 %collective-permute-start = (f32[2,64,256]{2,1,0:T(8,128)S(1)}, f32[2,64,256]{2,1,0:T(8,128)S(1)}, u32[]{:S(2)}, u32[]{:S(2)}) collective-permute-start(f32[2,64,256]{2,1,0:T(8,128)S(1)} %pad_maximum_fusion.3), channel_id=1, source_target_pairs={{0,8},{8,16},{16,24},{1,9},{9,17},{17,25},{2,10},{10,18},{18,26},{... | collective-permute-start | bytes 393224 | tf_op jit(solution)/shard_map/ppermute | solution.py:596
  7.4 1.3 collective-permute-start.1
  8.7 1.7 fusion.2
  10.4 1.7 fusion.3
  12.2 1.5 collective-permute-start.2
  13.8 1.3 collective-permute-start.3
  15.1 1.3 fusion.5
  17.0 1.5 broadcast_divide_fusion.kappa_ref
  18.7 1.3 pad_maximum_fusion.5.scal
  21.6 30.0 %residual_modes.1 = (f32[128,64,256]{2,1,0:T(8,128)}, f32[128,64,256]{2,1,0:T(8,128)}, f32[128,64,256]{2,1,0:T(8,128)}, f32[128,64,256]{2,1,0:T(8,128)}, f32[128...) custom-call(f32[19]{0:T(128)} %pad_maximum_fusion.5.scal, ...), custom_call_target="tpu_custom_call" | custom-call | tf_op jit(solution)/shard_map/residual_modes/pallas_call | solution.py:732
  51.5 13.0 %strip_borders.2 = f32[32,3,8,128]{3,2,1,0:T(8,128)} custom-call(f32[128,64,256]{2,1,0:T(8,128)} %get-tuple-element.24.modes_ref, f32[64,256]{1,0:T(8,128)} %get-tuple-element.25.ahead_ref, f32[64,256]{1,0:T(8,128)} %get-tuple-element.26.back_ref, f32[64,256]{1,0:T(8,128)} %constant.71.clone.decay_ref, f32[64,256]{1,0:T(8,128)} %constant.73.clone.border_ref), custom_call_target="tpu_custom_call" | custom-call | tf_op jit(solution)/shard_map/strip_borders/pallas_call | solution.py:613
  64.6 9.7 %all-to-all-start = ((f32[32,3,8,128]{3,2,1,0:T(8,128)}), f32[32,3,8,128]{3,2,1,0:T(8,128)S(1)}, u32[]{:S(2)}, u32[]{:S(2)}) async-start(f32[32,3,8,128]{3,2,1,0:T(8,128)} %strip_borders.2), calls=%async_computation | async-start | bytes 786432 | tf_op jit(solution)/shard_map/all_to_all | solution.py:630
  76.0 11.5 %all-to-all-done = f32[32,3,8,128]{3,2,1,0:T(8,128)S(1)} async-done(((f32[32,3,8,128]{3,2,1,0:T(8,128)}), f32[32,3,8,128]{3,2,1,0:T(8,128)S(1)}, u32[]{:S(2)}, u32[]{:S(2)}) %all-to-all-start) | async-done | bytes 393248 | tf_op jit(solution)/shard_map/all_to_all | solution.py:630
  88.2 6.0 %strip_faces.2 = f32[768,128]{1,0:T(8,128)} custom-call(s32[1]{0:T(128)} %bitcast.device, f32[768,128]{1,0:T(8,128)} %bitcast.26, f32[4,128,512]{2,1,0:T(8,128)} %constant.83.clone.table_ref, f32[32,56,512]{2,1,0:T(8,128)} %constant.82.clone.capacity_ref, f32[8,128,128]{2,1,0:T(8,128)} %pad_maximum_fusion.power_ref, ...), custom_call_target="tpu_custom_call" | custom-call | tf_op jit(solution)/shard_map/strip_faces/pallas_call | solution.py:635
  94.2 16.5 %all_to_all.20.faces_ref = f32[32,3,8,128]{3,2,1,0:T(8,128)} all-to-all(f32[32,3,8,128]{3,2,1,0:T(8,128)} %bitcast.27), channel_id=1, replica_groups=mesh['wide'=4,'narrow'=8] {'wide','narrow'}, dimensions={0} | all-to-all | bytes 786432 | tf_op jit(solution)/shard_map/all_to_all | solution.py:661
  110.7 19.4 %inverse_modes.2 = (f32[128,64,256]{2,1,0:T(8,128)}, f32[64,256]{1,0:T(8,128)}, f32[64,256]{1,0:T(8,128)}, f32[2,128,256]{2,1,0:T(8,128)}) custom-call(f32[32,3,8,128]{3,2,1,0:T(8,128)} %all_to_all.20.faces_ref, f32[128,64,256]{2,1,0:T(8,128)} %get-tuple-element.24.modes_ref, f32[64,256]{1,0:T(8,128)} %constant.71.clone.decay_ref, ...), custom_call_target="tpu_custom_call" | custom-call | tf_op jit(solution)/shard_map/inverse_modes/pallas_call | solution.py:680
  130.1 28.0 %image_modes.1 = (f32[128,64,256]{2,1,0:T(8,128)}, f32[128,64,256]{2,1,0:T(8,128)}, f32[64,256]{1,0:T(8,128)}, f32[64,256]{1,0:T(8,128)}, f32[5,8,256]{2,1,0:T(8,128)}) custom-call(f32[128,64,256]{2,1,0:T(8,128)} %get-tuple-element.27.field_ref.field_next.rest_3_, f32[128,64,256]{2,1,0:T(8,128)} %get-tuple-element.27.field_ref.field_next.rest_3_, ...), custom_call_target="tpu_custom_call" | custom-call | tf_op jit(solution)/shard_map/image_modes/pallas_call | solution.py:750
  158.2 13.6 %strip_borders.3 = f32[32,4,8,128]{3,2,1,0:T(8,128)} custom-call(f32[128,64,256]{2,1,0:T(8,128)} %get-tuple-element.37.modes_ref, f32[64,256]{1,0:T(8,128)} %get-tuple-element.38.ahead_ref, f32[64,256]{1,0:T(8,128)} %get-tuple-element.39.back_ref, f32[64,256]{1,0:T(8,128)} %constant.71.clone.decay_ref, f32[64,256]{1,0:T(8,128)} %constant.73.clone.border_ref, ...), custom_call_target="tpu_custom_call" | custom-call | tf_op jit(solution)/shard_map/strip_borders/pallas_call | solution.py:613
  171.8 18.8 %all_to_all.21 = f32[32,4,8,128]{3,2,1,0:T(8,128)} all-to-all(f32[32,4,8,128]{3,2,1,0:T(8,128)} %strip_borders.3), channel_id=1, replica_groups=mesh['wide'=4,'narrow'=8] {'wide','narrow'}, dimensions={0} | all-to-all | bytes 1048576 | tf_op jit(solution)/shard_map/all_to_all | solution.py:630
  190.6 6.2 %strip_faces.3 = f32[1024,128]{1,0:T(8,128)} custom-call(s32[1]{0:T(128)} %bitcast.device, f32[1024,128]{1,0:T(8,128)} %bitcast.24, f32[4,128,512]{2,1,0:T(8,128)} %constant.83.clone.table_ref, f32[32,56,512]{2,1,0:T(8,128)} %constant.82.clone.capacity_ref, f32[8,128,128]{2,1,0:T(8,128)} %pad_maximum_fusion.power_ref, ...), custom_call_target="tpu_custom_call" | custom-call | tf_op jit(solution)/shard_map/strip_faces/pallas_call | solution.py:635
  196.8 18.8 %all_to_all.22.faces_ref = f32[32,4,8,128]{3,2,1,0:T(8,128)} all-to-all(f32[32,4,8,128]{3,2,1,0:T(8,128)} %bitcast.25), channel_id=1, replica_groups=mesh['wide'=4,'narrow'=8] {'wide','narrow'}, dimensions={0} | all-to-all | bytes 1048576 | tf_op jit(solution)/shard_map/all_to_all | solution.py:661
  215.7 30.0 %inverse_modes.3 = (f32[128,64,256]{2,1,0:T(8,128)}, f32[128,64,256]{2,1,0:T(8,128)}, f32[128,64,256]{2,1,0:T(8,128)}) custom-call(f32[32,4,8,128]{3,2,1,0:T(8,128)} %all_to_all.22.faces_ref, f32[128,64,256]{2,1,0:T(8,128)} %get-tuple-element.37.modes_ref, f32[64,256]{1,0:T(8,128)} %constant.71.clone.decay_ref, f32[64,256]{1,0:T(8,128)} %constant.74.clone.scale_ref, ...), custom_call_target="tpu_custom_call" | custom-call | tf_op jit(solution)/shard_map/inverse_modes/pallas_call | solution.py:680
  (29 shorter events, 4.2 us)
Async XLA Ops:
  2.4 17.6 %collective-permute-start = (f32[2,64,256]{2,1,0:T(8,128)S(1)}, f32[2,64,256]{2,1,0:T(8,128)S(1)}, u32[]{:S(2)}, u32[]{:S(2)}) collective-permute-start(f32[2,64,256]{2,1,0:T(8,128)S(1)} %pad_maximum_fusion.3), channel_id=1, source_target_pairs={{0,8},{8,16},{16,24},{1,9},{9,17},{17,25},{2,10},{10,18},{18,26},{... | collective-permute-start | bytes 393224 | tf_op jit(solution)/shard_map/ppermute | solution.py:596
  7.4 12.7 %collective-permute-start.1 = (f32[2,64,256]{2,1,0:T(8,128)S(1)}, f32[2,64,256]{2,1,0:T(8,128)S(1)}, u32[]{:S(2)}, u32[]{:S(2)}) collective-permute-start(f32[2,64,256]{2,1,0:T(8,128)S(1)} %pad_maximum_fusion.4), channel_id=1, source_target_pairs={{8,0},{16,8},{24,16},{9,1},{17,9},{25,17},{10,2},{18,10},{26,18},{... | collective-permute-start | bytes 393224 | tf_op jit(solution)/shard_map/ppermute | solution.py:596
  12.2 7.9 %collective-permute-start.2 = (f32[2,128,256]{2,1,0:T(8,128)S(1)}, f32[2,128,256]{2,1,0:T(8,128)S(1)}, u32[]{:S(2)}, u32[]{:S(2)}) collective-permute-start(f32[2,128,256]{2,1,0:T(8,128)S(1)} %pad_maximum_fusion.1), channel_id=1, source_target_pairs={{0,1},{1,2},{2,3},{3,4},{4,5},{5,6},{6,7},{8,9},{9,10},{10,11},{11... | collective-permute-start | bytes 786440 | tf_op jit(solution)/shard_map/ppermute | solution.py:596
  13.8 6.3 %collective-permute-start.3 = (f32[2,128,256]{2,1,0:T(8,128)S(1)}, f32[2,128,256]{2,1,0:T(8,128)S(1)}, u32[]{:S(2)}, u32[]{:S(2)}) collective-permute-start(f32[2,128,256]{2,1,0:T(8,128)S(1)} %pad_maximum_fusion.2), channel_id=1, source_target_pairs={{1,0},{2,1},{3,2},{4,3},{5,4},{6,5},{7,6},{9,8},{10,9},{11,10},{12... | collective-permute-start | bytes 786440 | tf_op jit(solution)/shard_map/ppermute | solution.py:596
  20.1 0.6 copy-start.3
  20.1 0.7 copy-start.4
  20.1 0.8 copy-start.1
  20.9 0.7 copy-start.2
  64.6 22.9 %all-to-all-start = ((f32[32,3,8,128]{3,2,1,0:T(8,128)}), f32[32,3,8,128]{3,2,1,0:T(8,128)S(1)}, u32[]{:S(2)}, u32[]{:S(2)}) async-start(f32[32,3,8,128]{3,2,1,0:T(8,128)} %strip_borders.2), calls=%async_computation | async-start | bytes 786432 | tf_op jit(solution)/shard_map/all_to_all | solution.py:630
  87.5 0.7 copy-start

commit v3 on v2

v3 whole, which is shorter than its diff:
```python
import functools

import jax
import jax.numpy as jnp
import ml_dtypes
import numpy as np
from jax import lax
from jax.experimental import pallas as pl
from jax.experimental.pallas import tpu as pltpu
from jax.sharding import PartitionSpec as P

PHASES = 4
F32 = jnp.float32
BF16 = jnp.bfloat16
VMEM_LIMIT = 56 * 1024 * 1024
PLANES = 32
FORWARD_TERMS = ((0, 0), (0, 1), (1, 0), (1, 1), (0, 2), (2, 0))
INVERSE_TERMS = ((0, 0), (0, 1), (1, 0))


def cosine_table(length):
    m = np.arange(length)[:, None]
    n = np.arange(length)[None, :]
    weight = np.where(m == 0, np.sqrt(1.0 / length), np.sqrt(2.0 / length))
    return weight * np.cos(np.pi * (m * (2 * n + 1) % (4 * length)) / (2.0 * length))


def eigen_values(length):
    return 4.0 * np.sin(np.pi * np.arange(length) / (2.0 * length)) ** 2


def pieces(matrix, count=3):
    rest = np.asarray(matrix, np.float64)
    result = []
    for _ in range(count):
        piece = rest.astype(np.float32).astype(ml_dtypes.bfloat16)
        result.append(piece)
        rest = rest - piece.astype(np.float64)
    return np.stack(result)


def make_tables(size_x, size_y, size_z, wide, narrow):
    length_x = size_x * wide
    group = min(max(256 // size_y, 1), size_x)
    parity = np.concatenate([np.arange(0, size_y, 2), np.arange(1, size_y, 2)])
    strip = cosine_table(size_y)[parity]
    block_y = np.kron(np.eye(group), strip)
    table_z = cosine_table(size_z)
    shift = 4.0 * np.sin(np.pi / (2.0 * length_x)) ** 2
    eig_z = eigen_values(size_z)
    sigma = shift + eigen_values(size_y)[parity][:, None] + eig_z[None, :]
    theta = 2.0 * np.arcsinh(np.sqrt(sigma) / 2.0)
    decay = np.exp(-theta)
    square_rest = -np.expm1(-2.0 * theta)
    step = np.exp(-theta * size_x)
    total = -np.expm1(-2.0 * wide * size_x * theta)
    powers = np.stack([step**t / total for t in range(2 * wide)])
    border = np.broadcast_to(strip[:, :1], sigma.shape)
    eta = 2.0 * np.arcsinh(
        np.sqrt(shift + eig_z[:, None] + eigen_values(length_x)[None, :]) / 2.0
    )
    fade = np.exp(-eta * size_y)
    half_angle = np.pi * np.arange(1, narrow) / (2.0 * narrow)
    capacity = (np.tanh(eta / 2.0) * -np.expm1(-2.0 * eta * size_y))[None] / (
        (np.expm1(-eta * size_y) ** 2)[None]
        + 4.0 * fade[None] * (np.sin(half_angle) ** 2)[:, None, None]
    )
    devices = wide * narrow
    part = size_z // devices
    capacity = capacity.reshape(narrow - 1, devices, part, length_x).transpose(1, 0, 2, 3)
    k = np.arange(1, narrow)
    sines = np.sqrt(2.0 / narrow) * np.sin(np.pi * k[:, None] * k[None, :] / narrow)
    table_x = cosine_table(length_x).T.reshape(wide, size_x, length_x)
    by_mode = lambda left, right: np.concatenate([left.T, right.T], axis=1).reshape(devices, part, 2 * size_y)
    mix = np.stack(
        [
            np.stack(
                [
                    np.stack(
                        [
                            by_mode(powers[(d - 1 - b) % (2 * wide)], powers[(b - 1 - d) % (2 * wide)]),
                            by_mode(powers[(d + b) % (2 * wide)], powers[(2 * wide - 2 - b - d) % (2 * wide)]),
                        ],
                        axis=1,
                    )
                    for b in range(wide)
                ],
                axis=1,
            )
            for d in range(wide)
        ],
        axis=1,
    )
    even = np.broadcast_to((np.arange(size_y) < (size_y + 1) // 2)[:, None], sigma.shape)
    end = border * decay
    row = end / square_rest
    twice = lambda values: by_mode(values, values)
    f32 = lambda a: np.asarray(a, np.float32)
    return dict(
        group=group,
        planes=min(PLANES, size_x),
        z_fwd=pieces(table_z.T),
        z_inv=pieces(table_z, 2),
        y_fwd=pieces(block_y),
        y_inv=pieces(block_y.T, 2),
        theta=f32(theta.T.reshape(devices, part, size_y)),
        decay=f32(decay),
        border=f32(border),
        border_decay=f32(end),
        mix=f32(mix),
        row_even=f32(twice(np.where(even, row, 0.0))),
        row_odd=f32(twice(np.where(even, 0.0, row))),
        row_dot=f32(twice(1.0 / square_rest)),
        decay_inverse=f32(1.0 / decay),
        rest_inverse=f32(1.0 / square_rest),
        rest=f32(-np.expm1(-theta)),
        decay_rest=f32(decay / square_rest),
        mean_scale=float(np.sqrt(size_y * size_z) / (shift * decay[0, 0])),
        shift=float(shift),
        end_even=f32(twice(np.where(even, end, 0.0))),
        end_odd=f32(twice(np.where(even, 0.0, end))),
        capacity=f32(capacity.reshape(devices, (narrow - 1) * part, length_x)),
        sines=sines,
        table_x=f32(table_x),
    )


def split(values, count):
    result = [values.astype(BF16)]
    rest = values
    for _ in range(count - 1):
        rest = rest - result[-1].astype(F32)
        result.append(rest.astype(BF16))
    return result


def product_right(values, matrix_ref, terms):
    parts = split(values, 1 + max(a for a, _ in terms))
    total = None
    for a, b in reversed(terms):
        term = jnp.dot(parts[a], matrix_ref[b], preferred_element_type=F32)
        total = term if total is None else total + term
    return total


def product_left(matrix_ref, values, terms):
    parts = split(values, 1 + max(a for a, _ in terms))
    total = None
    for a, b in reversed(terms):
        term = jnp.dot(matrix_ref[b], parts[a], preferred_element_type=F32)
        total = term if total is None else total + term
    return total


def lookup(phase, scal, component):
    base = 4 * component
    picked = jnp.where(phase == 2.0, scal[base + 2], scal[base + 3])
    picked = jnp.where(phase == 1.0, scal[base + 1], picked)
    return jnp.where(phase == 0.0, scal[base], picked)


def forward_modes(first, block, base_inverse, z_ref, y_ref, decay_ref, sweep_ref, ahead_ref, back_ref, corner_ref, power):
    rows = block[0].shape[0]
    flat = jnp.concatenate(block, axis=0)
    flat = product_right(flat, z_ref, FORWARD_TERMS)
    flat = product_left(y_ref, flat, FORWARD_TERMS)
    decay = decay_ref[...]
    scale = decay * base_inverse
    ahead, back, weight, corner = (ahead_ref[...], back_ref[...], power[...], corner_ref[...])
    for j in range(len(block)):
        scaled = flat[j * rows : (j + 1) * rows] * scale
        ahead = decay * ahead + scaled
        sweep_ref[first + j] = ahead
        back = back + weight * scaled
        weight = weight * decay
        corner = corner + scaled[:8, :128]
    ahead_ref[...] = ahead
    back_ref[...] = back
    power[...] = weight
    corner_ref[...] = corner


def fold(values):
    rows, depth = values.shape
    return jnp.sum(values.reshape(rows // 8, 8, depth), axis=0)


def residual_kernel(
    group, planes,
    scal, phase_ref, phase_next, field_ref, field_next, x_before, x_after, y_before, y_after,
    z_mat, y_mat, decay_ref,
    residual_ref, sweep_ref, fx_ref, fy_ref, fz_ref, fx_low, fy_low, ahead_ref, back_ref, corner_ref,
    flux_low, power,
):
    step = pl.program_id(0)
    rows, depth = flux_low.shape
    gx, gy, gz = scal[12], scal[13], scal[14]
    flag_xb, flag_xa, flag_yb, flag_ya = scal[15], scal[16], scal[17], scal[18]
    row = lax.broadcasted_iota(jnp.int32, (rows, depth), 0)
    lane = lax.broadcasted_iota(jnp.int32, (rows, depth), 1)

    @pl.when(step == 0)
    def _():
        face = flag_xb / (lookup(x_before[0], scal, 0) + lookup(phase_ref[0].astype(F32), scal, 0))
        fx_low[...] = face
        flux_low[...] = face * (field_ref[0] - x_before[1] + gx)
        ahead_ref[...] = jnp.zeros_like(ahead_ref)
        back_ref[...] = jnp.zeros_like(back_ref)
        corner_ref[...] = jnp.zeros_like(corner_ref)
        power[...] = jnp.ones_like(power)

    last = step == pl.num_programs(0) - 1
    end_phase = jnp.where(last, x_after[0], phase_next[0].astype(F32))
    end_field = jnp.where(last, x_after[1], field_next[0])
    flag_end = jnp.where(last, flag_xa, 1.0)
    flux_x_low = flux_low[...]
    hx = lookup(phase_ref[0].astype(F32), scal, 0)
    done = []
    for j in range(planes):
        x = step * planes + j
        phase = phase_ref[j].astype(F32)
        field = field_ref[j]
        if j + 1 < planes:
            hx_next = lookup(phase_ref[j + 1].astype(F32), scal, 0)
            field_up = field_ref[j + 1]
            fx = 1.0 / (hx + hx_next)
        else:
            hx_next = lookup(end_phase, scal, 0)
            field_up = end_field
            fx = flag_end / (hx + hx_next)
        flux_x = fx * (field_up - field + gx)
        total = flux_x - flux_x_low
        flux_x_low, hx = flux_x, hx_next
        fx_ref[j] = fx

        hy = lookup(phase, scal, 1)
        hy_up = jnp.where(
            row == rows - 1,
            lookup(y_after[0, pl.ds(x, 1), :], scal, 1),
            pltpu.roll(hy, rows - 1, 0),
        )
        fy = jnp.where(row == rows - 1, flag_ya, 1.0) / (hy + hy_up)
        v_up = jnp.where(row == rows - 1, y_after[1, pl.ds(x, 1), :], pltpu.roll(field, rows - 1, 0))
        flux_y = fy * (v_up - field + gy)
        face = flag_yb / (lookup(y_before[0, pl.ds(x, 1), :], scal, 1) + hy[0:1])
        low = face * (field[0:1] - y_before[1, pl.ds(x, 1), :] + gy)
        total = total + (flux_y - jnp.where(row == 0, low, pltpu.roll(flux_y, 1, 0)))
        fy_ref[j] = fy
        fy_low[pl.ds(x, 1), :] = face

        hz = lookup(phase, scal, 2)
        fz = jnp.where(lane == depth - 1, 0.0, 1.0 / (hz + pltpu.roll(hz, depth - 1, 1)))
        flux_z = fz * (pltpu.roll(field, depth - 1, 1) - field + gz)
        total = total + (flux_z - pltpu.roll(flux_z, 1, 1))
        fz_ref[j] = fz
        residual_ref[j] = total
        done.append(total)
        if len(done) == group:
            forward_modes(
                j + 1 - group, done, scal[19], z_mat, y_mat, decay_ref, sweep_ref, ahead_ref, back_ref, corner_ref, power
            )
            done = []
    flux_low[...] = flux_x_low


def image_kernel(
    group, planes,
    scal, field_ref, field_next, fx_ref, fy_ref, fz_ref, fx_low, fy_low,
    x_jump, y_jump, z_mat, y_mat, decay_ref,
    image_ref, sweep_ref, ahead_ref, back_ref, corner_ref, sums_ref,
    flux_low, power,
):
    step = pl.program_id(0)
    rows, depth = flux_low.shape
    row = lax.broadcasted_iota(jnp.int32, (rows, depth), 0)

    @pl.when(step == 0)
    def _():
        flux_low[...] = fx_low[...] * x_jump[0]
        ahead_ref[...] = jnp.zeros_like(ahead_ref)
        back_ref[...] = jnp.zeros_like(back_ref)
        corner_ref[...] = jnp.zeros_like(corner_ref)
        power[...] = jnp.ones_like(power)
        sums_ref[...] = jnp.zeros_like(sums_ref)

    last = step == pl.num_programs(0) - 1
    end_jump = jnp.where(last, x_jump[1], field_next[0] - field_ref[planes - 1])
    flux_x_low = flux_low[...]
    sums = sums_ref[...]
    done = []
    for j in range(planes):
        x = step * planes + j
        field = field_ref[j]
        flux_x = fx_ref[j] * (field_ref[j + 1] - field if j + 1 < planes else end_jump)
        total = flux_x_low - flux_x
        flux_x_low = flux_x
        jump = jnp.where(row == rows - 1, y_jump[1, pl.ds(x, 1), :], pltpu.roll(field, rows - 1, 0) - field)
        flux_y = fy_ref[j] * jump
        low = fy_low[pl.ds(x, 1), :] * y_jump[0, pl.ds(x, 1), :]
        total = total + (jnp.where(row == 0, low, pltpu.roll(flux_y, 1, 0)) - flux_y)
        flux_z = fz_ref[j] * (pltpu.roll(field, depth - 1, 1) - field)
        total = total + (pltpu.roll(flux_z, 1, 1) - flux_z)
        image_ref[j] = total
        sums = sums + fold(field * total)
        done.append(total)
        if len(done) == group:
            forward_modes(
                j + 1 - group, done, scal[19], z_mat, y_mat, decay_ref, sweep_ref, ahead_ref, back_ref, corner_ref, power
            )
            done = []
    sums_ref[...] = sums
    flux_low[...] = flux_x_low


def local_kernel(
    devices, planes, summed,
    sweep_ref, ahead_ref, back_ref, corner_ref, decay_ref, border_ref, decay_inverse, decay_rest, *rest,
):
    if summed:
        sums_ref, earlier_ref, share_ref = rest[:3]
    out_ref, facts_ref, run, dots, rows_ref = rest[-5:]
    step = pl.program_id(0)
    blocks = pl.num_programs(0)
    decay = decay_ref[...]
    border = border_ref[...]
    half = decay.shape[0] // 2

    @pl.when(step == 0)
    def _():
        run[...] = ahead_ref[...] * decay_rest[...]
        dots[...] = jnp.zeros_like(dots)

    value, total = run[...], dots[...]
    first = (blocks - 1 - step) * planes
    for j in reversed(range(planes)):
        swept = sweep_ref[j]
        total = total + swept * swept
        value = swept + decay * value
        mode = value * border
        rows_ref[0, pl.ds(first + j, 1), :] = jnp.sum(mode[:half], axis=0, keepdims=True)
        rows_ref[1, pl.ds(first + j, 1), :] = jnp.sum(mode[half:], axis=0, keepdims=True)
    run[...] = value
    dots[...] = total

    @pl.when(step == blocks - 1)
    def _():
        part, width = out_ref.shape[2:]
        ahead = ahead_ref[...]
        ends = jnp.concatenate([ahead, back_ref[...]], axis=0)
        for slot, turned in enumerate((rows_ref[0].T, rows_ref[1].T, ends.T)):
            for j in range(devices):
                out_ref[j, slot] = turned[j * part : (j + 1) * part]
        lane = lax.broadcasted_iota(jnp.int32, facts_ref.shape, 1)
        square = jnp.sum(total * decay_inverse[...] + ahead * ahead * decay_rest[...])
        facts = jnp.where(lane == 0, square, 0.0) + jnp.where(lane == 1, jnp.sum(corner_ref[:1, :1]), 0.0)
        if summed:
            facts = facts + jnp.where(lane == 4, jnp.sum(sums_ref[...]), 0.0)
            facts = facts + pltpu.roll(earlier_ref[...] + share_ref[...], 2, 1)
        facts_ref[...] = facts


def faces_kernel(
    wide, narrow, part, sines, summed,
    device, got_ref, table_ref, capacity_ref, power_ref, mix_ref, row_even, row_odd, end_even, end_odd, row_dot,
    *rest,
):
    if summed:
        facts_ref, out_ref, jumps, modes = rest
    else:
        out_ref, share_ref, jumps, modes = rest
    devices = wide * narrow
    width = got_ref.shape[1]
    slots = 3
    out_slots = 4 if summed else 3
    faces = narrow - 1
    highest = dict(preferred_element_type=F32, precision=lax.Precision.HIGHEST)

    def take(ref, slot, mode, count):
        return ref[pl.ds(slot * part + mode, devices, stride=count * part), :]

    def incoming(ends, mode):
        swapped = pltpu.roll(ends, width // 2, 1)
        result = []
        for mine in range(wide):
            total = None
            for block in range(wide):
                at = slice(block * narrow, (block + 1) * narrow)
                term = mix_ref[0, mine, block, 0, pl.ds(mode, 1), :] * ends[at]
                term = term + mix_ref[0, mine, block, 1, pl.ds(mode, 1), :] * swapped[at]
                total = term if total is None else total + term
            result.append(total)
        return jnp.concatenate(result, axis=0)

    inner = None
    for mode in range(part):
        ends = take(got_ref, 2, mode, slots)
        entering = incoming(ends, mode)
        term = entering * pltpu.roll(ends, width // 2, 1) * row_dot[0, pl.ds(mode, 1), :]
        inner = term if inner is None else inner + term
        both = jnp.concatenate(
            [entering * row_even[0, pl.ds(mode, 1), :], entering * row_odd[0, pl.ds(mode, 1), :]], axis=0
        )
        added = jnp.dot(both, power_ref[mode], **highest)
        even = take(got_ref, 0, mode, slots) + added[:devices]
        odd = take(got_ref, 1, mode, slots) + added[devices:]
        jump = pltpu.roll(even + odd, devices - 1, 0) - (even - odd)
        jumps[pl.ds(mode, devices, stride=part), :] = jump
    mixed = None
    for block in range(wide):
        strips = [jumps[pl.ds((block * narrow + i) * part, part), :] for i in range(faces)]
        for k in range(faces):
            acc = None
            for i in range(faces):
                term = strips[i] * float(sines[k, i])
                acc = term if acc is None else acc + term
            modes[pl.ds(k * part, part), :] = acc
        term = jnp.dot(modes[...], table_ref[block], **highest)
        mixed = term if mixed is None else mixed + term
    plain = mixed
    mixed = mixed * capacity_ref[0]
    for block in range(wide):
        modes[...] = lax.dot_general(mixed, table_ref[block], (((1,), (1,)), ((), ())), **highest)
        solved = []
        for k in range(faces):
            acc = None
            for i in range(faces):
                term = modes[pl.ds(i * part, part), :] * float(sines[k, i])
                acc = term if acc is None else acc + term
            solved.append(acc)
        for strip in range(narrow):
            below = solved[strip - 1] if strip > 0 else jnp.zeros_like(solved[0])
            above = solved[strip] if strip < faces else jnp.zeros_like(solved[0])
            at = (block * narrow + strip) * out_slots * part
            out_ref[pl.ds(at, part), :] = above - below
            out_ref[pl.ds(at + part, part), :] = -(above + below)
    for mode in range(part):
        both = jnp.concatenate([take(out_ref, 0, mode, out_slots), take(out_ref, 1, mode, out_slots)], axis=0)
        added = lax.dot_general(both, power_ref[mode], (((1,), (1,)), ((), ())), **highest)
        added = pltpu.roll(added, width // 2, 1)
        ends = take(got_ref, 2, mode, slots) + end_even[0, pl.ds(mode, 1), :] * added[:devices]
        ends = ends + end_odd[0, pl.ds(mode, 1), :] * added[devices:]
        out_ref[pl.ds(2 * part + mode, devices, stride=out_slots * part), :] = incoming(ends, mode)
    share = jnp.sum(inner) - jnp.sum(plain * mixed)
    if summed:
        lane = lax.broadcasted_iota(jnp.int32, (part, width), 1)
        facts = facts_ref[:1, :width] + jnp.where(lane == 0, share, 0.0)
        for j in range(devices):
            out_ref[pl.ds((j * out_slots + 3) * part, part), :] = facts
    else:
        lane = lax.broadcasted_iota(jnp.int32, share_ref.shape, 1)
        share_ref[...] = jnp.where(lane == 0, share, 0.0)


def inverse_kernel(
    group, planes, dotted, voxels, mean_scale, shift,
    scal, faces_ref, sweep_ref, decay_ref, scale_ref, rest_inverse, decay_rest, rest_ref, y_mat, z_mat, *rest,
):
    if dotted:
        residual_ref, image_ref, along_ref, start_ref = rest[:4]
        out_ref, solution_ref, next_ref = rest[4:7]
    else:
        out_ref, jump_x, jump_y = rest[:3]
    run, added, rows_ref, entering, turned, factors = rest[-6:]
    step = pl.program_id(0)
    blocks = pl.num_programs(0)
    decay = decay_ref[...]
    rows, depth = decay.shape
    half = rows // 2

    @pl.when(step == 0)
    def _():
        devices, _, part, _ = faces_ref.shape
        for slot in range(3):
            for j in range(devices):
                turned[pl.ds(j * part, part), :] = faces_ref[j, slot]
            if slot < 2:
                rows_ref[slot] = turned[...].T
            else:
                entering[...] = turned[...].T
        scale = scale_ref[...]

        def body(x, value):
            face = jnp.concatenate(
                [
                    jnp.broadcast_to(rows_ref[0, pl.ds(x, 1), :], (half, depth)),
                    jnp.broadcast_to(rows_ref[1, pl.ds(x, 1), :], (half, depth)),
                ],
                axis=0,
            )
            value = decay * value + scale * face
            added[x] = value
            return value

        value = lax.fori_loop(0, blocks * planes, body, entering[pl.ds(0, rows), :], unroll=8)
        value = value + sweep_ref[planes - 1]
        beyond = decay_rest[...] * value + rest_inverse[...] * entering[pl.ds(rows, rows), :]
        run[...] = beyond
        if not dotted:
            entering[pl.ds(rows, rows), :] = rest_ref[...] * beyond - value

        if dotted:
            total = faces_ref[0, 3]
            for j in range(1, devices):
                total = total + faces_ref[j, 3]
            total = total[:1]
            lane = lax.broadcasted_iota(jnp.int32, total.shape, 1)
            pick = lambda i: jnp.sum(jnp.where(lane == i, total, 0.0), axis=1, keepdims=True)
            base = scal[20]

            def solved(square, constant):
                mean = constant * (mean_scale / voxels)
                field = constant * base * (mean_scale * shift)
                return mean, field, base * square - mean * field

            mean, image_sum, square = solved(pick(0), pick(1))
            mean_along, _, rz_now = solved(pick(2), pick(3))
            alpha = rz_now / (pick(4) - mean_along * image_sum)
            ratio = alpha * (alpha * square) / rz_now
            for i, factor in enumerate((alpha, mean_along, ratio, ratio * mean_along - alpha * mean)):
                factors[pl.ds(i, 1), :] = jnp.broadcast_to(factor, (1, depth))

    value = run[...]
    first = (blocks - 1 - step) * planes
    if dotted:
        alpha, mean, ratio, offset = [
            jnp.broadcast_to(factors[pl.ds(i, 1), :], (rows, depth)) for i in range(4)
        ]
    for start in reversed(range(0, planes, group)):
        modes = [None] * group
        for j in reversed(range(group)):
            value = (sweep_ref[start + j] + added[first + start + j]) + decay * value
            modes[j] = value
        flat = jnp.concatenate(modes, axis=0)
        flat = product_left(y_mat, flat, INVERSE_TERMS)
        flat = product_right(flat, z_mat, INVERSE_TERMS)
        for j in range(group):
            at = start + j
            plane = flat[j * rows : (j + 1) * rows]
            if dotted:
                along = along_ref[at]
                next_ref[at] = residual_ref[at] - alpha * image_ref[at]
                solution_ref[at] = start_ref[at] + alpha * (along - mean)
                plane = (ratio * along - offset) - alpha * plane
            out_ref[at] = plane
    run[...] = value

    if not dotted:
        @pl.when(step == blocks - 1)
        def _():
            before = rest_ref[...] * run[...] - entering[pl.ds(0, rows), :]
            flat = jnp.concatenate([before, entering[pl.ds(rows, rows), :]] * (group // 2), axis=0)
            flat = product_left(y_mat, flat, INVERSE_TERMS)
            flat = product_right(flat, z_mat, INVERSE_TERMS)
            jump_x[0] = flat[:rows]
            jump_x[1] = flat[rows : 2 * rows]
            jump_y[0] = product_right(-0.5 * (rows_ref[0] + rows_ref[1]), z_mat, INVERSE_TERMS)
            jump_y[1] = product_right(0.5 * (rows_ref[0] - rows_ref[1]), z_mat, INVERSE_TERMS)


def whole(shape, single=False):
    mode = dict(pipeline_mode=pl.Buffered(1)) if single else {}
    return pl.BlockSpec(shape, lambda *_: (0,) * len(shape), **mode)


def shape_of(*dims):
    return jax.ShapeDtypeStruct(dims, F32)


def params(dims):
    return pltpu.CompilerParams(dimension_semantics=("arbitrary",) * dims, vmem_limit_bytes=VMEM_LIMIT)


def neighbours(axis):
    devices = lax.axis_size(axis)
    up = [(i, i + 1) for i in range(devices - 1)]
    return up, [(j, i) for i, j in up]


def exchange(first, last, axis):
    up, down = neighbours(axis)
    return lax.ppermute(last, axis, up), lax.ppermute(first, axis, down)


def solve(forward, tab, device, scal, earlier=(), final=()):
    sweep, ahead, back, corner = forward
    size_x, size_y, size_z = sweep.shape
    wide, narrow = lax.axis_size("wide"), lax.axis_size("narrow")
    devices = wide * narrow
    group, planes = tab["group"], tab["planes"]
    blocks = size_x // planes
    part = size_z // devices
    plane = (size_y, size_z)
    block = (planes,) + plane
    summed = bool(final)
    field = shape_of(size_x, *plane)
    behind = pl.BlockSpec(block, lambda i: (blocks - 1 - i, 0, 0))
    packed = (devices, 3, part, size_x)
    sent, facts = pl.pallas_call(
        functools.partial(local_kernel, devices, planes, summed),
        grid=(blocks,),
        out_shape=(shape_of(*packed), shape_of(8, 128)),
        in_specs=[behind]
        + [whole(plane)] * 2
        + [whole((8, 128))]
        + [whole(plane)] * 4
        + [whole((8, size_z)), whole((8, 128)), whole((8, 128))] * summed,
        out_specs=(whole(packed), whole((8, 128))),
        scratch_shapes=[pltpu.VMEM(plane, F32), pltpu.VMEM(plane, F32), pltpu.VMEM((2, size_x, size_z), F32)],
        compiler_params=params(1),
        name="strip_borders",
    )(
        sweep, ahead, back, corner, tab["decay"], tab["border"], tab["decay_inverse"], tab["decay_rest"],
        *earlier,
    )
    got = lax.all_to_all(sent, ("wide", "narrow"), split_axis=0, concat_axis=0, tiled=True)
    faces = narrow - 1
    length_x = wide * size_x
    flat = (devices * 3 * part, size_x)
    out_slots = 4 if summed else 3
    flat_out = (devices * out_slots * part, size_x)
    small = (whole((8, 128)),)
    mine = lambda shape: pl.BlockSpec((1,) + shape, lambda i, idx: (idx[0],) + (0,) * len(shape))
    solved, *share = pl.pallas_call(
        functools.partial(faces_kernel, wide, narrow, part, tab["sines"], summed),
        out_shape=(shape_of(*flat_out),) + (shape_of(8, 128),) * (not summed),
        grid_spec=pltpu.PrefetchScalarGridSpec(
            num_scalar_prefetch=1,
            grid=(1,),
            in_specs=[
                whole(flat),
                whole((wide, size_x, length_x)),
                mine((faces * part, length_x)),
                whole((part, 2 * size_y, size_x)),
                mine((wide, wide, 2, part, size_x)),
            ]
            + [mine((part, size_x))] * 5
            + list(small) * summed,
            out_specs=(whole(flat_out),) + small * (not summed),
            scratch_shapes=[
                pltpu.VMEM((devices * part, size_x), F32),
                pltpu.VMEM((faces * part, size_x), F32),
            ],
        ),
        compiler_params=params(1),
        name="strip_faces",
    )(
        device, got.reshape(flat), tab["table_x"], tab["capacity"], tab["decay_powers"], tab["mix"],
        tab["row_even"], tab["row_odd"], tab["end_even"], tab["end_odd"], tab["row_dot"],
        *([facts] if summed else []),
    )
    mine_now = lax.all_to_all(
        solved.reshape(devices, out_slots, part, size_x), ("wide", "narrow"), split_axis=0, concat_axis=0, tiled=True
    )
    operands = [
        scal, mine_now, sweep, tab["decay"], tab["border_decay"], tab["rest_inverse"], tab["decay_rest"],
        tab["rest"], tab["y_inv"], tab["z_inv"],
    ]
    smem = pl.BlockSpec(memory_space=pltpu.SMEM)
    in_specs = [smem, whole(mine_now.shape), behind] + [whole(plane)] * 5
    in_specs += [whole(tab["y_inv"].shape), whole(tab["z_inv"].shape)]
    if summed:
        operands += final
        in_specs += [behind] * 4
        out_shape = (field,) * 3
        out_specs = (behind,) * 3
    else:
        jumps = (2, size_x, size_z)
        out_shape = (field, shape_of(2, *plane), shape_of(*jumps))
        out_specs = (behind, whole((2,) + plane), whole(jumps))
    voxels = float(devices * size_x * size_y * size_z)
    result = pl.pallas_call(
        functools.partial(inverse_kernel, group, planes, summed, voxels, tab["mean_scale"], tab["shift"]),
        grid=(blocks,),
        out_shape=out_shape,
        in_specs=in_specs,
        out_specs=out_specs,
        scratch_shapes=[
            pltpu.VMEM(plane, F32),
            pltpu.VMEM((size_x,) + plane, F32),
            pltpu.VMEM((2, size_x, size_z), F32),
            pltpu.VMEM((2 * size_y, size_z), F32),
            pltpu.VMEM((size_z, size_x), F32),
            pltpu.VMEM((8, size_z), F32),
        ],
        compiler_params=params(1),
        name="inverse_modes",
    )(*operands)
    return result, [facts, *share]


def on_device(phase_ids, conduct_table, gradient, start_field):
    size_x, size_y, size_z = start_field.shape
    wide, narrow = lax.axis_size("wide"), lax.axis_size("narrow")
    tab = make_tables(size_x, size_y, size_z, wide, narrow)
    tab = {k: jnp.asarray(v) if isinstance(v, np.ndarray) and k != "sines" else v for k, v in tab.items()}
    group, planes = tab["group"], tab["planes"]
    blocks = size_x // planes
    plane = (size_y, size_z)
    block = (planes,) + plane
    wide_at, narrow_at = lax.axis_index("wide"), lax.axis_index("narrow")
    device = (wide_at * narrow + narrow_at).astype(jnp.int32)
    theta = lax.dynamic_index_in_dim(tab["theta"], device, 0, False)[:, :, None]
    along_x = jnp.arange(size_x, dtype=F32)
    tab["decay_powers"] = jnp.concatenate(
        [jnp.exp(-theta * along_x), jnp.exp(-theta * (size_x - 1.0 - along_x))], axis=1
    )
    device = device.reshape(1)
    flags = jnp.stack([wide_at > 0, wide_at < wide - 1, narrow_at > 0, narrow_at < narrow - 1])
    base = jnp.mean(conduct_table).reshape(1)
    scal = jnp.concatenate([(0.5 / conduct_table).T.reshape(-1), gradient, flags.astype(F32), 1.0 / base, base])
    scal, tab["decay_powers"], device = lax.optimization_barrier((scal, tab["decay_powers"], device))

    edge = lambda dim, at: jnp.stack(
        [lax.index_in_dim(phase_ids, at, dim, False).astype(F32), lax.index_in_dim(start_field, at, dim, False)]
    )
    x_before, x_after = exchange(edge(0, 0), edge(0, size_x - 1), "wide")
    y_before, y_after = exchange(edge(1, 0), edge(1, size_y - 1), "narrow")

    main = pl.BlockSpec(block, lambda i: (i, 0, 0))
    following = pl.BlockSpec((1,) + plane, lambda i: (jnp.minimum((i + 1) * planes, size_x - 1), 0, 0))
    field_shape = shape_of(size_x, *plane)
    end_shapes = (shape_of(*plane),) * 2 + (shape_of(8, 128),)
    end_specs = (whole(plane),) * 2 + (whole((8, 128)),)
    matrices = [whole(tab["z_fwd"].shape), whole(tab["y_fwd"].shape), whole(plane)]
    carried = [pltpu.VMEM(plane, F32), pltpu.VMEM(plane, F32)]
    residual, sweep, fx, fy, fz, fx_low, fy_low, *ends = pl.pallas_call(
        functools.partial(residual_kernel, group, planes),
        grid=(blocks,),
        out_shape=(field_shape,) * 5 + (shape_of(*plane), shape_of(size_x, size_z)) + end_shapes,
        in_specs=[pl.BlockSpec(memory_space=pltpu.SMEM), main, following, main, following]
        + [whole((2,) + plane)] * 2
        + [whole((2, size_x, size_z))] * 2
        + matrices,
        out_specs=(main,) * 5 + (whole(plane), whole((size_x, size_z))) + end_specs,
        scratch_shapes=carried,
        compiler_params=params(1),
        name="residual_modes",
    )(
        scal, phase_ids, phase_ids, start_field, start_field, x_before, x_after, y_before, y_after,
        tab["z_fwd"], tab["y_fwd"], tab["decay"],
    )
    (along, jump_x, jump_y), earlier = solve((sweep, *ends), tab, device, scal)

    image, sweep, *ends, sums = pl.pallas_call(
        functools.partial(image_kernel, group, planes),
        grid=(blocks,),
        out_shape=(field_shape,) * 2 + end_shapes + (shape_of(8, size_z),),
        in_specs=[pl.BlockSpec(memory_space=pltpu.SMEM), main, following] + [main] * 3
        + [whole(plane), whole((size_x, size_z))]
        + [whole((2,) + plane), whole((2, size_x, size_z))]
        + matrices,
        out_specs=(main,) * 2 + end_specs + (whole((8, size_z)),),
        scratch_shapes=carried,
        compiler_params=params(1),
        name="image_modes",
    )(
        scal, along, along, fx, fy, fz, fx_low, fy_low, jump_x, jump_y,
        tab["z_fwd"], tab["y_fwd"], tab["decay"],
    )
    (new_direction, result, residual_next), _ = solve(
        (sweep, *ends), tab, device, scal, [sums, *earlier], [residual, image, along, start_field]
    )
    return result, residual_next, new_direction


def solution(mesh):
    placed = (P("wide", "narrow", None), P(), P(), P("wide", "narrow", None))
    return jax.shard_map(
        on_device,
        mesh=mesh,
        in_specs=placed,
        out_specs=(P("wide", "narrow", None),) * 3,
        check_vma=False,
    )
```

time: 247 us -> 216 us (0.87)
  Pallas kernels: 146 us -> 119 us
  blocking collectives: 54.2 us -> 74.8 us
  waiting for transfers between devices: 11.5 us -> 0.01 us
  starting transfers between devices: 18.7 us -> 8.99 us
  other arithmetic: 6.81 us -> 4.02 us
    all_to_all x1 -> x2, blocking collectives: 18.8 us -> 39.5 us  [solve(): lax.all_to_all(sent, ('wide', 'narrow'), split_axis=0, concat_axis=0, til...]
    pallas_call x2, Pallas kernels: 26.7 us -> 12.5 us  [solve(): pl.pallas_call(functools.partial(local_kernel, devices, planes, summed),...]
    all_to_all x1 -> x0, waiting for transfers between devices: 11.5 us -> none  [solve(): lax.all_to_all(sent, ('wide', 'narrow'), split_axis=0, concat_axis=0, til...]
    pallas_call x2, Pallas kernels: 49.4 us -> 39.4 us  [solve(): pl.pallas_call(functools.partial(inverse_kernel, group, planes, summed, v...]
    all_to_all x1 -> x0, starting transfers between devices: 9.71 us -> none  [solve(): lax.all_to_all(sent, ('wide', 'narrow'), split_axis=0, concat_axis=0, til...]
    pallas_call x1, Pallas kernels: 28 us -> 25.2 us  [on_device(): pl.pallas_call(functools.partial(image_kernel, group, planes), grid=(bloc...]
  transfers between devices with their start and end apart: 5 -> 4, of which waited for: 1 -> 0; matrix products, arithmetic and copies ran while one was open for 4% -> 4% of each run, Pallas kernels for 0% -> 0%
where the time goes in v3:
time: 216 us; the launch traced here: 215 us
  Pallas kernels  119 us (55%)
  blocking collectives  74.8 us (35%)
  starting transfers between devices  8.99 us (4%)
  local copies, waits for them, and re-layouts  7.33 us (3%)
  other arithmetic  4.02 us (2%)
    all_to_all x2, blocking collectives, solve(): lax.all_to_all(sent, ('wide', 'narrow'), split_axis=0, concat_axis=0, til...  39.5 us
    pallas_call x2, Pallas kernels, solve(): pl.pallas_call(functools.partial(inverse_kernel, group, planes, summed, v...  39.4 us
    all_to_all x2, blocking collectives, solve(): lax.all_to_all(solved.reshape(devices, out_slots, part, size_x), ('wide',...  35.3 us
    pallas_call x1, Pallas kernels, on_device(): pl.pallas_call(functools.partial(residual_kernel, group, planes), grid=(b...  29.5 us
    pallas_call x1, Pallas kernels, on_device(): pl.pallas_call(functools.partial(image_kernel, group, planes), grid=(bloc...  25.2 us
    pallas_call x2, Pallas kernels, solve(): pl.pallas_call(functools.partial(local_kernel, devices, planes, summed),...  12.5 us
    pallas_call x2, Pallas kernels, solve(): pl.pallas_call(functools.partial(faces_kernel, wide, narrow, part, tab['s...  12.1 us
    ppermute x4, starting transfers between devices, exchange(): return (lax.ppermute(last, axis, up), lax.ppermute(first, axis, down))  8.99 us
  transfers between devices with their start and end apart: 4, of which 0 were waited for; matrix products, arithmetic and copies ran while one was open for 4% of the time, Pallas kernels for 0%

profile of v3, /device:TPU:0, one launch (start us, length us, event | category | flops | bytes accessed | tf_op | source)
XLA Modules:
  0.0 215.4 jit_solution(9940181915961052127)
XLA Ops:
  0.6 0.9 slice_convert_fusion
  1.5 0.9 fusion.4
  2.4 4.9 %collective-permute-start = (f32[2,64,256]{2,1,0:T(8,128)S(1)}, f32[2,64,256]{2,1,0:T(8,128)S(1)}, u32[]{:S(2)}, u32[]{:S(2)}) collective-permute-start(f32[2,64,256]{2,1,0:T(8,128)S(1)} %pad_maximum_fusion.3), channel_id=1, source_target_pairs={{0,8},{8,16},{16,24},{1,9},{9,17},{17,25},{2,10},{10,18},{18,26},{... | collective-permute-start | bytes 393224 | tf_op jit(solution)/shard_map/ppermute | solution.py:581
  7.4 1.3 collective-permute-start.1
  8.7 1.7 fusion.2
  10.4 1.7 fusion.3
  12.2 1.5 collective-permute-start.2
  13.8 1.3 collective-permute-start.3
  15.1 0.7 negate_bitcast_fusion
  15.9 1.3 fusion.5
  18.2 1.3 concatenate.6.scal
  19.5 0.8 pad_maximum_fusion.power_ref
  21.8 29.5 %residual_modes.1 = (f32[128,64,256]{2,1,0:T(8,128)}, f32[128,64,256]{2,1,0:T(8,128)}, f32[128,64,256]{2,1,0:T(8,128)}, f32[128,64,256]{2,1,0:T(8,128)}, f32[128...) custom-call(f32[21]{0:T(128)} %concatenate.6.scal, ...), custom_call_target="tpu_custom_call" | custom-call | tf_op jit(solution)/shard_map/residual_modes/pallas_call | solution.py:726
  51.4 6.2 %strip_borders.2 = (f32[32,3,8,128]{3,2,1,0:T(8,128)}, f32[8,128]{1,0:T(8,128)}) custom-call(f32[128,64,256]{2,1,0:T(8,128)} %get-tuple-element.36.sweep_ref, f32[64,256]{1,0:T(8,128)} %get-tuple-element.37.ahead_ref, f32[64,256]{1,0:T(8,128)} %get-tuple-element.38.back_ref, f32[8,128]{1,0:T(8,128)} %get-tuple-element.39.corner_ref, ...), custom_call_target="tpu_custom_call" | custom-call | tf_op jit(solution)/shard_map/strip_borders/pallas_call | solution.py:598
  57.6 23.0 %all_to_all.20 = f32[32,3,8,128]{3,2,1,0:T(8,128)} all-to-all(f32[32,3,8,128]{3,2,1,0:T(8,128)} %get-tuple-element.40), channel_id=1, replica_groups=mesh['wide'=4,'narrow'=8] {'wide','narrow'}, dimensions={0} | all-to-all | bytes 786432 | tf_op jit(solution)/shard_map/all_to_all | solution.py:615
  80.6 6.0 %strip_faces.2 = (f32[768,128]{1,0:T(8,128)}, f32[8,128]{1,0:T(8,128)}) custom-call(s32[1]{0:T(128)} %bitcast.7.device, f32[768,128]{1,0:T(8,128)} %bitcast.26, f32[4,128,512]{2,1,0:T(8,128)} %constant.91.clone.table_ref, f32[32,56,512]{2,1,0:T(8,128)} %constant.90.clone.capacity_ref, f32[8,128,128]{2,1,0:T(8,128)} %pad_maximum_fusion.power_ref, ...), custom_call_target="tpu_custom_call" | custom-call | tf_op jit(solution)/shard_map/strip_faces/pallas_call | solution.py:623
  86.6 16.5 %all_to_all.21.faces_ref = f32[32,3,8,128]{3,2,1,0:T(8,128)} all-to-all(f32[32,3,8,128]{3,2,1,0:T(8,128)} %bitcast.29), channel_id=1, replica_groups=mesh['wide'=4,'narrow'=8] {'wide','narrow'}, dimensions={0} | all-to-all | bytes 786432 | tf_op jit(solution)/shard_map/all_to_all | solution.py:651
  103.1 14.0 %inverse_modes.2 = (f32[128,64,256]{2,1,0:T(8,128)}, f32[2,64,256]{2,1,0:T(8,128)}, f32[2,128,256]{2,1,0:T(8,128)}) custom-call(f32[21]{0:T(128)} %concatenate.6.scal, f32[32,3,8,128]{3,2,1,0:T(8,128)} %all_to_all.21.faces_ref, f32[128,64,256]{2,1,0:T(8,128)} %get-tuple-element.36.sweep_ref, f32[64,256]{1,0:T(8,128)} %constant.77.clone.decay_ref, ...), custom_call_target="tpu_custom_call" | custom-call | tf_op jit(solution)/shard_map/inverse_modes/pallas_call | solution.py:671
  117.1 25.2 %image_modes.1 = (f32[128,64,256]{2,1,0:T(8,128)}, f32[128,64,256]{2,1,0:T(8,128)}, f32[64,256]{1,0:T(8,128)}, f32[64,256]{1,0:T(8,128)}, f32[8,128]{1,0:T(8,128)}, /*index=5*/f32[8,256]{1,0:T(8,128)}) custom-call(f32[21]{0:T(128)} %concatenate.6.scal, f32[128,64,256]{2,1,0:T(8,128)} %get-tuple-element.43.field_ref.field_next.rest_2_, ...), custom_call_target="tpu_custom_call" | custom-call | tf_op jit(solution)/shard_map/image_modes/pallas_call | solution.py:744
  142.3 6.3 %strip_borders.3 = (f32[32,3,8,128]{3,2,1,0:T(8,128)}, f32[8,128]{1,0:T(8,128)}) custom-call(f32[128,64,256]{2,1,0:T(8,128)} %get-tuple-element.51.sweep_ref, f32[64,256]{1,0:T(8,128)} %get-tuple-element.52.ahead_ref, f32[64,256]{1,0:T(8,128)} %get-tuple-element.53.back_ref, f32[8,128]{1,0:T(8,128)} %get-tuple-element.54.corner_ref, ...), custom_call_target="tpu_custom_call" | custom-call | tf_op jit(solution)/shard_map/strip_borders/pallas_call | solution.py:598
  148.6 16.5 %all_to_all.22 = f32[32,3,8,128]{3,2,1,0:T(8,128)} all-to-all(f32[32,3,8,128]{3,2,1,0:T(8,128)} %get-tuple-element.58), channel_id=1, replica_groups=mesh['wide'=4,'narrow'=8] {'wide','narrow'}, dimensions={0} | all-to-all | bytes 786432 | tf_op jit(solution)/shard_map/all_to_all | solution.py:615
  165.0 6.1 %strip_faces.3 = f32[1024,128]{1,0:T(8,128)} custom-call(s32[1]{0:T(128)} %bitcast.7.device, f32[768,128]{1,0:T(8,128)} %bitcast.25, f32[4,128,512]{2,1,0:T(8,128)} %constant.91.clone.table_ref, f32[32,56,512]{2,1,0:T(8,128)} %constant.90.clone.capacity_ref, f32[8,128,128]{2,1,0:T(8,128)} %pad_maximum_fusion.power_ref, ...), custom_call_target="tpu_custom_call" | custom-call | tf_op jit(solution)/shard_map/strip_faces/pallas_call | solution.py:623
  171.1 18.8 %all_to_all.23.faces_ref = f32[32,4,8,128]{3,2,1,0:T(8,128)} all-to-all(f32[32,4,8,128]{3,2,1,0:T(8,128)} %bitcast.24), channel_id=1, replica_groups=mesh['wide'=4,'narrow'=8] {'wide','narrow'}, dimensions={0} | all-to-all | bytes 1048576 | tf_op jit(solution)/shard_map/all_to_all | solution.py:651
  190.0 25.4 %inverse_modes.3 = (f32[128,64,256]{2,1,0:T(8,128)}, f32[128,64,256]{2,1,0:T(8,128)}, f32[128,64,256]{2,1,0:T(8,128)}) custom-call(f32[21]{0:T(128)} %concatenate.6.scal, f32[32,4,8,128]{3,2,1,0:T(8,128)} %all_to_all.23.faces_ref, f32[128,64,256]{2,1,0:T(8,128)} %get-tuple-element.51.sweep_ref, f32[64,256]{1,0:T(8,128)} %constant.77.clone.decay_ref, ...), custom_call_target="tpu_custom_call" | custom-call | tf_op jit(solution)/shard_map/inverse_modes/pallas_call | solution.py:671
  (25 shorter events, 2.0 us)
Async XLA Ops:
  2.4 17.9 %collective-permute-start = (f32[2,64,256]{2,1,0:T(8,128)S(1)}, f32[2,64,256]{2,1,0:T(8,128)S(1)}, u32[]{:S(2)}, u32[]{:S(2)}) collective-permute-start(f32[2,64,256]{2,1,0:T(8,128)S(1)} %pad_maximum_fusion.3), channel_id=1, source_target_pairs={{0,8},{8,16},{16,24},{1,9},{9,17},{17,25},{2,10},{10,18},{18,26},{... | collective-permute-start | bytes 393224 | tf_op jit(solution)/shard_map/ppermute | solution.py:581
  7.4 13.0 %collective-permute-start.1 = (f32[2,64,256]{2,1,0:T(8,128)S(1)}, f32[2,64,256]{2,1,0:T(8,128)S(1)}, u32[]{:S(2)}, u32[]{:S(2)}) collective-permute-start(f32[2,64,256]{2,1,0:T(8,128)S(1)} %pad_maximum_fusion.4), channel_id=1, source_target_pairs={{8,0},{16,8},{24,16},{9,1},{17,9},{25,17},{10,2},{18,10},{26,18},{... | collective-permute-start | bytes 393224 | tf_op jit(solution)/shard_map/ppermute | solution.py:581
  12.2 8.1 %collective-permute-start.2 = (f32[2,128,256]{2,1,0:T(8,128)S(1)}, f32[2,128,256]{2,1,0:T(8,128)S(1)}, u32[]{:S(2)}, u32[]{:S(2)}) collective-permute-start(f32[2,128,256]{2,1,0:T(8,128)S(1)} %pad_maximum_fusion.1), channel_id=1, source_target_pairs={{0,1},{1,2},{2,3},{3,4},{4,5},{5,6},{6,7},{8,9},{9,10},{10,11},{11... | collective-permute-start | bytes 786440 | tf_op jit(solution)/shard_map/ppermute | solution.py:581
  13.8 6.6 %collective-permute-start.3 = (f32[2,128,256]{2,1,0:T(8,128)S(1)}, f32[2,128,256]{2,1,0:T(8,128)S(1)}, u32[]{:S(2)}, u32[]{:S(2)}) collective-permute-start(f32[2,128,256]{2,1,0:T(8,128)S(1)} %pad_maximum_fusion.2), channel_id=1, source_target_pairs={{1,0},{2,1},{3,2},{4,3},{5,4},{6,5},{7,6},{9,8},{10,9},{11,10},{12... | collective-permute-start | bytes 786440 | tf_op jit(solution)/shard_map/ppermute | solution.py:581
  20.3 0.7 copy-start.2
  20.4 0.7 copy-start.3
  20.4 0.8 copy-start
  21.2 0.7 copy-start.1

commit v4 on v3

--- a/solution.py
+++ b/solution.py
@@ -14,8 +14,8 @@
 BF16 = jnp.bfloat16
 VMEM_LIMIT = 56 * 1024 * 1024
 PLANES = 32
-FORWARD_TERMS = ((0, 0), (0, 1), (1, 0), (1, 1), (0, 2), (2, 0))
-INVERSE_TERMS = ((0, 0), (0, 1), (1, 0))
+FULL_TERMS = ((0, 0), (0, 1), (1, 0), (1, 1), (0, 2), (2, 0))
+SHORT_TERMS = ((0, 0), (0, 1), (1, 0))
 
 
 def cosine_table(length):
@@ -99,10 +99,10 @@
     return dict(
         group=group,
         planes=min(PLANES, size_x),
-        z_fwd=pieces(table_z.T),
-        z_inv=pieces(table_z, 2),
-        y_fwd=pieces(block_y),
-        y_inv=pieces(block_y.T, 2),
+        z_fwd=pieces(table_z.T, 2),
+        z_inv=pieces(table_z),
+        y_fwd=pieces(block_y, 2),
+        y_inv=pieces(block_y.T),
         theta=f32(theta.T.reshape(devices, part, size_y)),
         decay=f32(decay),
         border=f32(border),
@@ -162,8 +162,8 @@
 def forward_modes(first, block, base_inverse, z_ref, y_ref, decay_ref, sweep_ref, ahead_ref, back_ref, corner_ref, power):
     rows = block[0].shape[0]
     flat = jnp.concatenate(block, axis=0)
-    flat = product_right(flat, z_ref, FORWARD_TERMS)
-    flat = product_left(y_ref, flat, FORWARD_TERMS)
+    flat = product_right(flat, z_ref, SHORT_TERMS)
+    flat = product_left(y_ref, flat, SHORT_TERMS)
     decay = decay_ref[...]
     scale = decay * base_inverse
     ahead, back, weight, corner = (ahead_ref[...], back_ref[...], power[...], corner_ref[...])
@@ -461,6 +461,7 @@
     else:
         out_ref, jump_x, jump_y = rest[:3]
     run, added, rows_ref, entering, turned, factors = rest[-6:]
+    terms = SHORT_TERMS if dotted else FULL_TERMS
     step = pl.program_id(0)
     blocks = pl.num_programs(0)
     decay = decay_ref[...]
@@ -531,8 +532,8 @@
             value = (sweep_ref[start + j] + added[first + start + j]) + decay * value
             modes[j] = value
         flat = jnp.concatenate(modes, axis=0)
-        flat = product_left(y_mat, flat, INVERSE_TERMS)
-        flat = product_right(flat, z_mat, INVERSE_TERMS)
+        flat = product_left(y_mat, flat, terms)
+        flat = product_right(flat, z_mat, terms)
         for j in range(group):
             at = start + j
             plane = flat[j * rows : (j + 1) * rows]
@@ -549,12 +550,12 @@
         def _():
             before = rest_ref[...] * run[...] - entering[pl.ds(0, rows), :]
             flat = jnp.concatenate([before, entering[pl.ds(rows, rows), :]] * (group // 2), axis=0)
-            flat = product_left(y_mat, flat, INVERSE_TERMS)
-            flat = product_right(flat, z_mat, INVERSE_TERMS)
+            flat = product_left(y_mat, flat, terms)
+            flat = product_right(flat, z_mat, terms)
             jump_x[0] = flat[:rows]
             jump_x[1] = flat[rows : 2 * rows]
-            jump_y[0] = product_right(-0.5 * (rows_ref[0] + rows_ref[1]), z_mat, INVERSE_TERMS)
-            jump_y[1] = product_right(0.5 * (rows_ref[0] - rows_ref[1]), z_mat, INVERSE_TERMS)
+            jump_y[0] = product_right(-0.5 * (rows_ref[0] + rows_ref[1]), z_mat, terms)
+            jump_y[1] = product_right(0.5 * (rows_ref[0] - rows_ref[1]), z_mat, terms)
 
 
 def whole(shape, single=False):
@@ -593,13 +594,14 @@
     block = (planes,) + plane
     summed = bool(final)
     field = shape_of(size_x, *plane)
+    long = min(2 * planes, size_x)
     behind = pl.BlockSpec(block, lambda i: (blocks - 1 - i, 0, 0))
     packed = (devices, 3, part, size_x)
     sent, facts = pl.pallas_call(
-        functools.partial(local_kernel, devices, planes, summed),
-        grid=(blocks,),
+        functools.partial(local_kernel, devices, long, summed),
+        grid=(size_x // long,),
         out_shape=(shape_of(*packed), shape_of(8, 128)),
-        in_specs=[behind]
+        in_specs=[pl.BlockSpec((long,) + plane, lambda i: (size_x // long - 1 - i, 0, 0))]
         + [whole(plane)] * 2
         + [whole((8, 128))]
         + [whole(plane)] * 4

time: 216 us -> 217 us (level)
    pallas_call x2, Pallas kernels: 39.4 us -> 47 us  [solve(): pl.pallas_call(functools.partial(inverse_kernel, group, planes, summed, v...]
    pallas_call x1, Pallas kernels: 29.5 us -> 26.7 us  [on_device(): pl.pallas_call(functools.partial(residual_kernel, group, planes), grid=(b...]
    pallas_call x1, Pallas kernels: 25.2 us -> 22.4 us  [on_device(): pl.pallas_call(functools.partial(image_kernel, group, planes), grid=(bloc...]
where the time goes in v4:
time: 217 us; the launch traced here: 216 us
  Pallas kernels  120 us (55%)
  blocking collectives  74.8 us (34%)
  starting transfers between devices  8.99 us (4%)
  local copies, waits for them, and re-layouts  7.33 us (3%)
  other arithmetic  4.02 us (2%)
    pallas_call x2, Pallas kernels, solve(): pl.pallas_call(functools.partial(inverse_kernel, group, planes, summed, v...  47 us
    all_to_all x2, blocking collectives, solve(): lax.all_to_all(sent, ('wide', 'narrow'), split_axis=0, concat_axis=0, til...  39.5 us
    all_to_all x2, blocking collectives, solve(): lax.all_to_all(solved.reshape(devices, out_slots, part, size_x), ('wide',...  35.3 us
    pallas_call x1, Pallas kernels, on_device(): pl.pallas_call(functools.partial(residual_kernel, group, planes), grid=(b...  26.7 us
    pallas_call x1, Pallas kernels, on_device(): pl.pallas_call(functools.partial(image_kernel, group, planes), grid=(bloc...  22.4 us
    pallas_call x2, Pallas kernels, solve(): pl.pallas_call(functools.partial(faces_kernel, wide, narrow, part, tab['s...  12.1 us
    pallas_call x2, Pallas kernels, solve(): pl.pallas_call(functools.partial(local_kernel, devices, long, summed), gr...  11.4 us
    ppermute x4, starting transfers between devices, exchange(): return (lax.ppermute(last, axis, up), lax.ppermute(first, axis, down))  8.99 us
  transfers between devices with their start and end apart: 4, of which 0 were waited for; matrix products, arithmetic and copies ran while one was open for 4% of the time, Pallas kernels for 0%

profile of v4, /device:TPU:0, one launch (start us, length us, event | category | flops | bytes accessed | tf_op | source)
XLA Modules:
  0.0 216.4 jit_solution(3294277119189565208)
XLA Ops:
  0.6 0.9 slice_convert_fusion
  1.5 0.9 fusion.4
  2.4 4.9 %collective-permute-start = (f32[2,64,256]{2,1,0:T(8,128)S(1)}, f32[2,64,256]{2,1,0:T(8,128)S(1)}, u32[]{:S(2)}, u32[]{:S(2)}) collective-permute-start(f32[2,64,256]{2,1,0:T(8,128)S(1)} %pad_maximum_fusion.3), channel_id=1, source_target_pairs={{0,8},{8,16},{16,24},{1,9},{9,17},{17,25},{2,10},{10,18},{18,26},{... | collective-permute-start | bytes 393224 | tf_op jit(solution)/shard_map/ppermute | solution.py:582
  7.4 1.3 collective-permute-start.1
  8.7 1.7 fusion.2
  10.4 1.7 fusion.3
  12.2 1.5 collective-permute-start.2
  13.8 1.3 collective-permute-start.3
  15.1 0.7 negate_bitcast_fusion
  15.9 1.3 fusion.5
  18.2 1.3 concatenate.6.scal
  19.5 0.8 pad_maximum_fusion.power_ref
  21.8 26.7 %residual_modes.1 = (f32[128,64,256]{2,1,0:T(8,128)}, f32[128,64,256]{2,1,0:T(8,128)}, f32[128,64,256]{2,1,0:T(8,128)}, f32[128,64,256]{2,1,0:T(8,128)}, f32[128...) custom-call(f32[21]{0:T(128)} %concatenate.6.scal, ...), custom_call_target="tpu_custom_call" | custom-call | tf_op jit(solution)/shard_map/residual_modes/pallas_call | solution.py:728
  48.6 5.7 %strip_borders.2 = (f32[32,3,8,128]{3,2,1,0:T(8,128)}, f32[8,128]{1,0:T(8,128)}) custom-call(f32[128,64,256]{2,1,0:T(8,128)} %get-tuple-element.36.sweep_ref, f32[64,256]{1,0:T(8,128)} %get-tuple-element.37.ahead_ref, f32[64,256]{1,0:T(8,128)} %get-tuple-element.38.back_ref, f32[8,128]{1,0:T(8,128)} %get-tuple-element.39.corner_ref, ...), custom_call_target="tpu_custom_call" | custom-call | tf_op jit(solution)/shard_map/strip_borders/pallas_call | solution.py:600
  54.3 23.0 %all_to_all.20 = f32[32,3,8,128]{3,2,1,0:T(8,128)} all-to-all(f32[32,3,8,128]{3,2,1,0:T(8,128)} %get-tuple-element.40), channel_id=1, replica_groups=mesh['wide'=4,'narrow'=8] {'wide','narrow'}, dimensions={0} | all-to-all | bytes 786432 | tf_op jit(solution)/shard_map/all_to_all | solution.py:617
  77.3 6.0 %strip_faces.2 = (f32[768,128]{1,0:T(8,128)}, f32[8,128]{1,0:T(8,128)}) custom-call(s32[1]{0:T(128)} %bitcast.7.device, f32[768,128]{1,0:T(8,128)} %bitcast.26, f32[4,128,512]{2,1,0:T(8,128)} %constant.91.clone.table_ref, f32[32,56,512]{2,1,0:T(8,128)} %constant.90.clone.capacity_ref, f32[8,128,128]{2,1,0:T(8,128)} %pad_maximum_fusion.power_ref, ...), custom_call_target="tpu_custom_call" | custom-call | tf_op jit(solution)/shard_map/strip_faces/pallas_call | solution.py:625
  83.3 16.5 %all_to_all.21.faces_ref = f32[32,3,8,128]{3,2,1,0:T(8,128)} all-to-all(f32[32,3,8,128]{3,2,1,0:T(8,128)} %bitcast.29), channel_id=1, replica_groups=mesh['wide'=4,'narrow'=8] {'wide','narrow'}, dimensions={0} | all-to-all | bytes 786432 | tf_op jit(solution)/shard_map/all_to_all | solution.py:653
  99.7 21.5 %inverse_modes.2 = (f32[128,64,256]{2,1,0:T(8,128)}, f32[2,64,256]{2,1,0:T(8,128)}, f32[2,128,256]{2,1,0:T(8,128)}) custom-call(f32[21]{0:T(128)} %concatenate.6.scal, f32[32,3,8,128]{3,2,1,0:T(8,128)} %all_to_all.21.faces_ref, f32[128,64,256]{2,1,0:T(8,128)} %get-tuple-element.36.sweep_ref, f32[64,256]{1,0:T(8,128)} %constant.77.clone.decay_ref, ...), custom_call_target="tpu_custom_call" | custom-call | tf_op jit(solution)/shard_map/inverse_modes/pallas_call | solution.py:673
  121.3 22.4 %image_modes.1 = (f32[128,64,256]{2,1,0:T(8,128)}, f32[128,64,256]{2,1,0:T(8,128)}, f32[64,256]{1,0:T(8,128)}, f32[64,256]{1,0:T(8,128)}, f32[8,128]{1,0:T(8,128)}, /*index=5*/f32[8,256]{1,0:T(8,128)}) custom-call(f32[21]{0:T(128)} %concatenate.6.scal, f32[128,64,256]{2,1,0:T(8,128)} %get-tuple-element.43.field_ref.field_next.rest_2_, ...), custom_call_target="tpu_custom_call" | custom-call | tf_op jit(solution)/shard_map/image_modes/pallas_call | solution.py:746
  143.7 5.7 %strip_borders.3 = (f32[32,3,8,128]{3,2,1,0:T(8,128)}, f32[8,128]{1,0:T(8,128)}) custom-call(f32[128,64,256]{2,1,0:T(8,128)} %get-tuple-element.51.sweep_ref, f32[64,256]{1,0:T(8,128)} %get-tuple-element.52.ahead_ref, f32[64,256]{1,0:T(8,128)} %get-tuple-element.53.back_ref, f32[8,128]{1,0:T(8,128)} %get-tuple-element.54.corner_ref, ...), custom_call_target="tpu_custom_call" | custom-call | tf_op jit(solution)/shard_map/strip_borders/pallas_call | solution.py:600
  149.4 16.5 %all_to_all.22 = f32[32,3,8,128]{3,2,1,0:T(8,128)} all-to-all(f32[32,3,8,128]{3,2,1,0:T(8,128)} %get-tuple-element.58), channel_id=1, replica_groups=mesh['wide'=4,'narrow'=8] {'wide','narrow'}, dimensions={0} | all-to-all | bytes 786432 | tf_op jit(solution)/shard_map/all_to_all | solution.py:617
  165.9 6.1 %strip_faces.3 = f32[1024,128]{1,0:T(8,128)} custom-call(s32[1]{0:T(128)} %bitcast.7.device, f32[768,128]{1,0:T(8,128)} %bitcast.25, f32[4,128,512]{2,1,0:T(8,128)} %constant.91.clone.table_ref, f32[32,56,512]{2,1,0:T(8,128)} %constant.90.clone.capacity_ref, f32[8,128,128]{2,1,0:T(8,128)} %pad_maximum_fusion.power_ref, ...), custom_call_target="tpu_custom_call" | custom-call | tf_op jit(solution)/shard_map/strip_faces/pallas_call | solution.py:625
  172.0 18.8 %all_to_all.23.faces_ref = f32[32,4,8,128]{3,2,1,0:T(8,128)} all-to-all(f32[32,4,8,128]{3,2,1,0:T(8,128)} %bitcast.24), channel_id=1, replica_groups=mesh['wide'=4,'narrow'=8] {'wide','narrow'}, dimensions={0} | all-to-all | bytes 1048576 | tf_op jit(solution)/shard_map/all_to_all | solution.py:653
  190.9 25.5 %inverse_modes.3 = (f32[128,64,256]{2,1,0:T(8,128)}, f32[128,64,256]{2,1,0:T(8,128)}, f32[128,64,256]{2,1,0:T(8,128)}) custom-call(f32[21]{0:T(128)} %concatenate.6.scal, f32[32,4,8,128]{3,2,1,0:T(8,128)} %all_to_all.23.faces_ref, f32[128,64,256]{2,1,0:T(8,128)} %get-tuple-element.51.sweep_ref, f32[64,256]{1,0:T(8,128)} %constant.77.clone.decay_ref, ...), custom_call_target="tpu_custom_call" | custom-call | tf_op jit(solution)/shard_map/inverse_modes/pallas_call | solution.py:673
  (25 shorter events, 2.0 us)
Async XLA Ops:
  2.4 17.9 %collective-permute-start = (f32[2,64,256]{2,1,0:T(8,128)S(1)}, f32[2,64,256]{2,1,0:T(8,128)S(1)}, u32[]{:S(2)}, u32[]{:S(2)}) collective-permute-start(f32[2,64,256]{2,1,0:T(8,128)S(1)} %pad_maximum_fusion.3), channel_id=1, source_target_pairs={{0,8},{8,16},{16,24},{1,9},{9,17},{17,25},{2,10},{10,18},{18,26},{... | collective-permute-start | bytes 393224 | tf_op jit(solution)/shard_map/ppermute | solution.py:582
  7.4 13.0 %collective-permute-start.1 = (f32[2,64,256]{2,1,0:T(8,128)S(1)}, f32[2,64,256]{2,1,0:T(8,128)S(1)}, u32[]{:S(2)}, u32[]{:S(2)}) collective-permute-start(f32[2,64,256]{2,1,0:T(8,128)S(1)} %pad_maximum_fusion.4), channel_id=1, source_target_pairs={{8,0},{16,8},{24,16},{9,1},{17,9},{25,17},{10,2},{18,10},{26,18},{... | collective-permute-start | bytes 393224 | tf_op jit(solution)/shard_map/ppermute | solution.py:582
  12.2 8.1 %collective-permute-start.2 = (f32[2,128,256]{2,1,0:T(8,128)S(1)}, f32[2,128,256]{2,1,0:T(8,128)S(1)}, u32[]{:S(2)}, u32[]{:S(2)}) collective-permute-start(f32[2,128,256]{2,1,0:T(8,128)S(1)} %pad_maximum_fusion.1), channel_id=1, source_target_pairs={{0,1},{1,2},{2,3},{3,4},{4,5},{5,6},{6,7},{8,9},{9,10},{10,11},{11... | collective-permute-start | bytes 786440 | tf_op jit(solution)/shard_map/ppermute | solution.py:582
  13.8 6.6 %collective-permute-start.3 = (f32[2,128,256]{2,1,0:T(8,128)S(1)}, f32[2,128,256]{2,1,0:T(8,128)S(1)}, u32[]{:S(2)}, u32[]{:S(2)}) collective-permute-start(f32[2,128,256]{2,1,0:T(8,128)S(1)} %pad_maximum_fusion.2), channel_id=1, source_target_pairs={{1,0},{2,1},{3,2},{4,3},{5,4},{6,5},{7,6},{9,8},{10,9},{11,10},{12... | collective-permute-start | bytes 786440 | tf_op jit(solution)/shard_map/ppermute | solution.py:582
  20.3 0.7 copy-start.2
  20.4 0.7 copy-start.3
  20.4 0.8 copy-start
  21.2 0.7 copy-start.1
